TPU v7x, 256 devices: a whole 4x4x8 slice. The times are simulated.
256 devices in a mesh: tm: 128 (over x, z, y), rep: 2 (over core).
Axes of the slice: x: 4, y: 4, z: 8, core: 2. Of those that a mesh axis runs over, the one named last changes fastest.
Arguments:
- table: bfloat16 [2, 32768, 512], P(None, 'tm'), may hold values from -30 to 30
- cotangent: bfloat16 [2, 32768, 512], P(None, 'tm'), may hold values from -6 to 6
- stamps: int32 [2, 32768], P(None, 'tm'), may hold values from 0 to 98304, as said below
- starts: int32 [2, 32768], P(None, 'tm'), may hold values from 0 to 65535, as said below
- w_query: bfloat16 [512, 512], P(None, 'rep'), may hold values from -0.5 to 0.5
- w_key: bfloat16 [512, 512], P(None, 'rep'), may hold values from -0.5 to 0.5
- w_value: bfloat16 [512, 512], P(None, 'rep'), may hold values from -0.25 to 0.25
- w_out: bfloat16 [512, 512], P('rep'), may hold values from -0.25 to 0.25
- decay: float32 [4], P('rep'), may hold values from 0.0002 to 0.02
Outputs:
- mixed: bfloat16 [2, 32768, 512], P(None, 'tm')
- grad_table: bfloat16 [2, 32768, 512], P(None, 'tm')
- grad_query: float32 [512, 512], P(None, 'rep')
- grad_key: float32 [512, 512], P(None, 'rep')
- grad_value: float32 [512, 512], P(None, 'rep')
- grad_out: float32 [512, 512], P('rep')
Inputs may be any that keep to these rules, and one draw needn't show every extreme that they name: In time order the stamps never fall, successive rows differ by 0 to 3, the first row has stamp 0 and the last row has stamp 3 * 32768. For the row r in time order, starts lies between max(0, (r // 256 - 2) * 256) and r; the first row of each block reaches the lower end and the last row of each block starts at itself.
All inputs are finite; a program needn't handle non-finite values.
Results may differ from a plain program's by a relative error of at most 0.0045.
The roundings to bfloat16 on the way count: a program that leaves them out, or rounds other values in their place, can miss the bound.
Values may be sent and summed in bfloat16 or wider, within the bound.
A program may use at most 64 MiB of HBM per device.

v0:
```python
import math

import jax
import jax.numpy as jnp
from jax import lax
from jax.sharding import PartitionSpec as P

HD = 128


def for_sending(shard):

    def short(part):
        return part.astype(jnp.bfloat16) if part.dtype == jnp.float32 else part

    return jax.tree.map(short, shard)


def passed_along(block, axis, distance):
    devices = range(lax.axis_size(axis))
    route = [(i - distance, i) for i in devices if i - distance in devices]
    return lax.ppermute(block, axis, route)


def attend(q_rows, window, key_times, q_times, q_first, first_blk, decay, grad_attn):
    blk_rows = q_rows.shape[0]
    head_cols = q_rows.shape[1]
    head_count = head_cols // HD
    inv_scale = 1.0 / math.sqrt(HD)
    q_heads = q_rows.reshape(blk_rows, head_count, HD)
    k_heads = window[:, :head_cols].reshape(3 * blk_rows, head_count, HD)
    v_heads = window[:, head_cols:].reshape(3 * blk_rows, head_count, HD)
    g_heads = grad_attn.reshape(blk_rows, head_count, HD)
    q_pos = first_blk * blk_rows + jnp.arange(blk_rows, dtype=jnp.int32)
    k_pos = (first_blk - 2) * blk_rows + jnp.arange(3 * blk_rows, dtype=jnp.int32)
    allowed = (k_pos[None, :] >= q_first[:, None]) & (k_pos[None, :] <= q_pos[:, None])
    time_gap = (q_times[:, None] - key_times[None, :]).astype(jnp.float32)
    scores = (
        jnp.einsum("qhd,khd->hqk", q_heads, k_heads, preferred_element_type=jnp.float32) * inv_scale
    )
    scores = scores - decay[:, None, None] * time_gap[None]
    scores = jnp.where(allowed[None], scores, -1e30)
    row_max = jnp.max(scores, -1, keepdims=True)
    weights = jnp.where(allowed[None], jnp.exp(scores - row_max), 0.0)
    probs = weights / jnp.sum(weights, -1, keepdims=True)
    probs_low = probs.astype(jnp.bfloat16)
    attn = jnp.einsum(
        "hqk,khd->qhd", probs_low, v_heads, preferred_element_type=jnp.float32
    ).astype(jnp.bfloat16)
    d_probs = jnp.einsum("qhd,khd->hqk", g_heads, v_heads, preferred_element_type=jnp.float32)
    delta = jnp.sum(probs * d_probs, -1, keepdims=True)
    d_scores = (probs * (d_probs - delta)).astype(jnp.bfloat16)
    d_query = (
        jnp.einsum("hqk,khd->qhd", d_scores, k_heads, preferred_element_type=jnp.float32)
        * inv_scale
    ).astype(jnp.bfloat16)
    d_key = (
        jnp.einsum("hqk,qhd->khd", d_scores, q_heads, preferred_element_type=jnp.float32)
        * inv_scale
    )
    d_value = jnp.einsum("hqk,qhd->khd", probs_low, g_heads, preferred_element_type=jnp.float32)
    d_window = jnp.concatenate(
        [d_key.reshape(3 * blk_rows, head_cols), d_value.reshape(3 * blk_rows, head_cols)], 1
    )
    return (attn.reshape(blk_rows, head_cols), d_query.reshape(blk_rows, head_cols), d_window)


def shards(table, cotangent, stamps, starts, w_query, w_key, w_value, w_out, decay):
    tm_size = lax.axis_size("tm")
    dev_index = lax.axis_index("tm")
    blk_rows = table.shape[1]
    width = table.shape[2]
    head_cols = w_query.shape[1]
    flat_rows = table.reshape(2 * blk_rows, width)
    flat_grad = cotangent.reshape(2 * blk_rows, width)
    queries = jnp.dot(flat_rows, w_query, preferred_element_type=jnp.float32).astype(jnp.bfloat16)
    key_rows = jnp.dot(flat_rows, w_key, preferred_element_type=jnp.float32).astype(jnp.bfloat16)
    val_rows = jnp.dot(flat_rows, w_value, preferred_element_type=jnp.float32).astype(jnp.bfloat16)
    packed = jnp.concatenate([key_rows, val_rows], 1).reshape(2, blk_rows, 2 * head_cols)
    grad_attn = jnp.dot(flat_grad, w_out.T, preferred_element_type=jnp.float32).astype(jnp.bfloat16)
    nearby = {}
    for offset in (1, 2, -1, -2):
        nearby[offset] = passed_along(for_sending((packed, stamps)), "tm", offset)

    def pick(offset, which):
        got = nearby[offset]
        return (got[0][which], got[1][which])

    low_m2 = pick(2, 0)
    low_m1 = pick(1, 0)
    high_p2 = pick(-2, 1)
    edge_low = pick(-1, 0)
    edge_high = pick(-1, 1)
    top_fold = dev_index <= tm_size - 3
    at_second = dev_index == tm_size - 2
    at_last = dev_index == tm_size - 1
    before_last = dev_index <= tm_size - 2
    low_window = jnp.concatenate([low_m2[0], low_m1[0], packed[0]], 0)
    low_times = jnp.concatenate([low_m2[1], low_m1[1], stamps[0]], 0)
    high_two = jnp.where(top_fold, high_p2[0], jnp.where(at_second, edge_low[0], low_m1[0]))
    high_two_t = jnp.where(top_fold, high_p2[1], jnp.where(at_second, edge_low[1], low_m1[1]))
    high_one = jnp.where(before_last, edge_high[0], packed[0])
    high_one_t = jnp.where(before_last, edge_high[1], stamps[0])
    high_window = jnp.concatenate([high_two, high_one, packed[1]], 0)
    high_times = jnp.concatenate([high_two_t, high_one_t, stamps[1]], 0)
    low_attn, low_dq, low_dwin = attend(
        queries[:blk_rows],
        low_window,
        low_times,
        stamps[0],
        starts[0],
        dev_index,
        decay,
        grad_attn[:blk_rows],
    )
    high_attn, high_dq, high_dwin = attend(
        queries[blk_rows:],
        high_window,
        high_times,
        stamps[1],
        starts[1],
        2 * tm_size - 1 - dev_index,
        decay,
        grad_attn[blk_rows:],
    )
    attn_all = jnp.concatenate([low_attn, high_attn], 0)
    dq_all = jnp.concatenate([low_dq, high_dq], 0)
    partial_out = jnp.dot(attn_all, w_out, preferred_element_type=jnp.float32)
    mixed = lax.psum(partial_out, "rep").astype(jnp.bfloat16).reshape(2, blk_rows, width)
    low_two, low_one, low_own = (
        low_dwin[:blk_rows],
        low_dwin[blk_rows : 2 * blk_rows],
        low_dwin[2 * blk_rows :],
    )
    hi_two, hi_one, hi_own = (
        high_dwin[:blk_rows],
        high_dwin[blk_rows : 2 * blk_rows],
        high_dwin[2 * blk_rows :],
    )
    zero_blk = jnp.zeros_like(low_own)
    near_one = low_one + jnp.where(at_last, hi_two, 0.0)
    far_two = jnp.where(top_fold, hi_two, 0.0)
    grad_near = {}
    grad_near[-1] = jnp.stack(
        [jnp.where(at_second, hi_two, 0.0), jnp.where(before_last, hi_one, 0.0)]
    )
    grad_near[2] = jnp.stack([low_two, zero_blk])
    grad_near[1] = jnp.stack([near_one, zero_blk])
    grad_near[-2] = jnp.stack([zero_blk, far_two])
    grad_own = jnp.stack([low_own + jnp.where(at_last, hi_one, 0.0), hi_own])
    for offset in (1, 2, -1, -2):
        grad_own = grad_own + passed_along(grad_near[offset], "tm", -offset)
    grad_own = grad_own.reshape(2 * blk_rows, 2 * head_cols)
    dk_all = grad_own[:, :head_cols].astype(jnp.bfloat16)
    dv_all = grad_own[:, head_cols:].astype(jnp.bfloat16)
    partial_in = (
        jnp.dot(dq_all, w_query.T, preferred_element_type=jnp.float32)
        + jnp.dot(dk_all, w_key.T, preferred_element_type=jnp.float32)
        + jnp.dot(dv_all, w_value.T, preferred_element_type=jnp.float32)
    )
    grad_table = lax.psum(partial_in, "rep").astype(jnp.bfloat16).reshape(2, blk_rows, width)
    grad_scale = 1.0 / math.sqrt(2 * blk_rows * tm_size)
    contract = (((0,), (0,)), ((), ()))
    term_query = (
        lax.dot_general(flat_rows, dq_all, contract, preferred_element_type=jnp.float32)
        * grad_scale
    )
    term_key = (
        lax.dot_general(flat_rows, dk_all, contract, preferred_element_type=jnp.float32)
        * grad_scale
    )
    term_value = (
        lax.dot_general(flat_rows, dv_all, contract, preferred_element_type=jnp.float32)
        * grad_scale
    )
    term_out = (
        lax.dot_general(attn_all, flat_grad, contract, preferred_element_type=jnp.float32)
        * grad_scale
    )
    grad_query, grad_key, grad_value, grad_out = lax.psum(
        (term_query, term_key, term_value, term_out), "tm"
    )
    return (mixed, grad_table, grad_query, grad_key, grad_value, grad_out)


def solution(mesh):
    return jax.shard_map(
        shards,
        mesh=mesh,
        in_specs=(
            P(None, "tm", None),
            P(None, "tm", None),
            P(None, "tm"),
            P(None, "tm"),
            P(None, "rep"),
            P(None, "rep"),
            P(None, "rep"),
            P("rep", None),
            P("rep"),
        ),
        out_specs=(
            P(None, "tm", None),
            P(None, "tm", None),
            P(None, "rep"),
            P(None, "rep"),
            P(None, "rep"),
            P("rep", None),
        ),
        check_vma=False,
    )
```

profile of v0, /device:TPU:32, one launch (start us, length us, event | category | flops | bytes accessed | tf_op | source)
XLA Modules:
  0.0 410.3 jit_solution(2229600774342179052)
XLA Ops:
  8.2 1.3 convolution_convert_fusion.2
  9.5 1.3 convolution_convert_fusion.3
  11.3 4.5 %collective-permute-start.5 = (bf16[2,256,512]{1,2,0:T(8,128)(2,1)S(1)}, bf16[2,256,512]{1,2,0:T(8,128)(2,1)}, u32[]{:S(2)}, u32[]{:S(2)}) collective-permute-start(bf16[2,256,512]{1,2,0:T(8,128)(2,1)S(1)} %copy.27), channel_id=1, source_target_pairs={{2,0},{4,2},{6,4},{8,6},{10,8},{12,10},{14,12},{16,14},{18,16},{20... | collective-permute-start | bytes 1572872 | tf_op jit(solution)/shard_map/ppermute | solution.py:22
  15.8 1.9 collective-permute-start.1
  17.8 4.1 %collective-permute-start.4 = (bf16[2,256,512]{1,2,0:T(8,128)(2,1)S(1)}, bf16[2,256,512]{1,2,0:T(8,128)(2,1)}, u32[]{:S(2)}, u32[]{:S(2)}) collective-permute-start(bf16[2,256,512]{1,2,0:T(8,128)(2,1)S(1)} %copy.27), channel_id=1, source_target_pairs={{4,0},{6,2},{8,4},{10,6},{12,8},{14,10},{16,12},{18,14},{20,16},{2... | collective-permute-start | bytes 1572872 | tf_op jit(solution)/shard_map/ppermute | solution.py:22
  21.9 4.7 %collective-permute-start.6 = (s32[2,256]{1,0:T(2,128)S(1)}, s32[2,256]{1,0:T(2,128)S(1)}, u32[]{:S(2)}, u32[]{:S(2)}) collective-permute-start(s32[2,256]{1,0:T(2,128)S(1)} %copy-done.24), channel_id=1, source_target_pairs={{4,0},{6,2},{8,4},{10,6},{12,8},{14,10},{16,12},{18,14},{20,16},{2... | collective-permute-start | bytes 6152 | tf_op jit(solution)/shard_map/ppermute | solution.py:22
  26.6 1.9 collective-permute-start.7
  32.5 7.5 %collective-permute-done.7 = s32[2,256]{1,0:T(2,128)S(1)} collective-permute-done((s32[2,256]{1,0:T(2,128)S(1)}, s32[2,256]{1,0:T(2,128)S(1)}, u32[]{:S(2)}, u32[]{:S(2)}) %collective-permute-start.7) | collective-permute-done | bytes 2080 | tf_op jit(solution)/shard_map/ppermute | solution.py:22
  40.0 1.9 collective-permute-start.3
  42.0 2.6 collective-permute-done.6
  44.6 5.8 %collective-permute-start = (bf16[2,256,512]{1,2,0:T(8,128)(2,1)S(1)}, bf16[2,256,512]{1,2,0:T(8,128)(2,1)S(1)}, u32[]{:S(2)}, u32[]{:S(2)}) collective-permute-start(bf16[2,256,512]{1,2,0:T(8,128)(2,1)S(1)} %copy.27), channel_id=1, source_target_pairs={{0,4},{2,6},{4,8},{6,10},{8,12},{10,14},{12,16},{14,18},{16,20},{1... | collective-permute-start | bytes 1572872 | tf_op jit(solution)/shard_map/ppermute | solution.py:22
  50.4 2.9 collective-permute-start.2
  53.3 8.1 %collective-permute-done.2 = s32[2,256]{1,0:T(2,128)S(1)} collective-permute-done((s32[2,256]{1,0:T(2,128)S(1)}, s32[2,256]{1,0:T(2,128)S(1)}, u32[]{:S(2)}, u32[]{:S(2)}) %collective-permute-start.2) | collective-permute-done | bytes 2080 | tf_op jit(solution)/shard_map/ppermute | solution.py:22
  64.5 1.4 fusion.31
  66.8 3.5 fusion.58
  70.3 2.0 multiply_reduce_fusion
  73.6 1.2 fusion.23
  75.6 3.4 fusion.59
  79.0 1.9 fusion.26
  83.9 4.7 %collective-permute-start.11 = (f32[2,256,512]{1,2,0:T(8,128)S(1)}, f32[2,256,512]{1,2,0:T(8,128)S(1)}, u32[]{:S(2)}, u32[]{:S(2)}) collective-permute-start(f32[2,256,512]{1,2,0:T(8,128)S(1)} %stack.47), channel_id=1, source_target_pairs={{0,4},{2,6},{4,8},{6,10},{8,12},{10,14},{12,16},{14,18},{16,20},{1... | collective-permute-start | bytes 3145736 | tf_op jit(solution)/shard_map/ppermute | solution.py:22
  88.6 1.9 collective-permute-start.10
  90.7 3.7 collective-permute-start.9
  94.5 4.7 %collective-permute-start.8 = (f32[2,256,512]{1,2,0:T(8,128)S(1)}, f32[2,256,512]{1,2,0:T(8,128)S(1)}, u32[]{:S(2)}, u32[]{:S(2)}) collective-permute-start(f32[2,256,512]{1,2,0:T(8,128)S(1)} %stack.40), channel_id=1, source_target_pairs={{2,0},{4,2},{6,4},{8,6},{10,8},{12,10},{14,12},{16,14},{18,16},{20... | collective-permute-start | bytes 3145736 | tf_op jit(solution)/shard_map/ppermute | solution.py:22
  102.4 32.2 %collective-permute-done.11 = f32[2,256,512]{1,2,0:T(8,128)S(1)} collective-permute-done((f32[2,256,512]{1,2,0:T(8,128)S(1)}, f32[2,256,512]{1,2,0:T(8,128)S(1)}, u32[]{:S(2)}, u32[]{:S(2)}) %collective-permute-start.11) | collective-permute-done | bytes 1048608 | tf_op jit(solution)/shard_map/ppermute | solution.py:22
  134.6 19.1 %collective-permute-done.10 = f32[2,256,512]{1,2,0:T(8,128)S(1)} collective-permute-done((f32[2,256,512]{1,2,0:T(8,128)S(1)}, f32[2,256,512]{1,2,0:T(8,128)S(1)}, u32[]{:S(2)}, u32[]{:S(2)}) %collective-permute-start.10) | collective-permute-done | bytes 1048608 | tf_op jit(solution)/shard_map/ppermute | solution.py:22
  153.7 2.4 collective-permute-done.9
  156.1 10.4 %collective-permute-done.8 = f32[2,256,512]{1,2,0:T(8,128)S(1)} collective-permute-done((f32[2,256,512]{1,2,0:T(8,128)S(1)}, f32[2,256,512]{1,2,0:T(8,128)S(1)}, u32[]{:S(2)}, u32[]{:S(2)}) %collective-permute-start.8) | collective-permute-done | bytes 1048608 | tf_op jit(solution)/shard_map/ppermute | solution.py:22
  167.1 1.1 fusion.5
  172.0 9.3 %all-reduce.9 = (bf16[512,512]{1,0:T(8,128)(2,1)}, bf16[512,512]{1,0:T(8,128)(2,1)}) all-reduce(f32[512,512]{1,0:T(8,128)S(1)} %fusion.39, f32[512,512]{1,0:T(8,128)S(1)} %convolution_add_fusion), channel_id=1, replica_groups=mesh['tm'=128,'rep'=2] {'rep'}, use_global_device_ids=true, to_apply=%region_4.5 | all-reduce | flops 524288 | bytes 3145728 | tf_op jit(solution)/shard_map/psum | solution.py:129
  181.2 216.2 %all-reduce.8.cloned.1.call-done = (f32[512,256]{0,1:T(8,128)}, f32[512,256]{0,1:T(8,128)}, f32[512,256]{0,1:T(8,128)}, f32[256,512]{1,0:T(8,128)}) async-done(((f32[512,256]{0,1:T(8,128)}, f32[512,256]{0,1:T(8,128)}, f32[512,256]{0,1:T(8,128)}, f32[256,512]{1,0:T(8,128)}), (f32[512,256]{0,1:T(8,128)}, f32[512,256]{0,1:T(8,128)}, f32[512,256]{0,1:T(8,128)}, ...) | async-done | bytes 2097168 | tf_op jit(solution)/shard_map/psum | solution.py:180
  397.5 2.1 copy.40
  399.6 2.0 copy.41
  (115 shorter events, 23.7 us)
Async XLA Ops:
  7.2 1.0 copy-start
  7.2 390.3 %all-reduce.8.cloned.1.call-start = ((), (), s32[]{:S(2)}) async-start(), calls=%async_computation | async-start | bytes 4194304 | tf_op jit(solution)/shard_map/psum | solution.py:180
  10.8 11.0 %copy-start.24 = (s32[2,256]{1,0:T(2,128)S(1)}, s32[2,256]{1,0:T(2,128)}, u32[]{:S(2)}) copy-start(s32[2,256]{1,0:T(2,128)} %param.11) | copy-start | bytes 6148
  10.8 17.7 %copy-start.8 = (bf16[512,256]{1,0:T(8,128)(2,1)S(1)}, bf16[512,256]{1,0:T(8,128)(2,1)}, u32[]{:S(2)}) copy-start(bf16[512,256]{1,0:T(8,128)(2,1)} %param.13) | copy-start | bytes 786436
  11.1 18.5 %copy-start.23 = (s32[2,256]{1,0:T(2,128)S(1)}, s32[2,256]{1,0:T(2,128)}, u32[]{:S(2)}) copy-start(s32[2,256]{1,0:T(2,128)} %param.12) | copy-start | bytes 6148
  11.1 18.5 %copy-start.1 = (bf16[2,256,512]{2,1,0:T(8,128)(2,1)S(1)}, bf16[2,256,512]{2,1,0:T(8,128)(2,1)}, u32[]{:S(2)}) copy-start(bf16[2,256,512]{2,1,0:T(8,128)(2,1)} %param.10) | copy-start | bytes 1572868
  11.1 18.5 %copy-start.7 = (bf16[256,512]{1,0:T(8,128)(2,1)S(1)}, bf16[256,512]{1,0:T(8,128)(2,1)}, u32[]{:S(2)}) copy-start(bf16[256,512]{1,0:T(8,128)(2,1)} %param.16) | copy-start | bytes 786436
  11.3 53.1 %collective-permute-start.5 = (bf16[2,256,512]{1,2,0:T(8,128)(2,1)S(1)}, bf16[2,256,512]{1,2,0:T(8,128)(2,1)}, u32[]{:S(2)}, u32[]{:S(2)}) collective-permute-start(bf16[2,256,512]{1,2,0:T(8,128)(2,1)S(1)} %copy.27), channel_id=1, source_target_pairs={{2,0},{4,2},{6,4},{8,6},{10,8},{12,10},{14,12},{16,14},{18,16},{20... | collective-permute-start | bytes 1572872 | tf_op jit(solution)/shard_map/ppermute | solution.py:22
  15.8 47.6 %collective-permute-start.1 = (bf16[2,256,512]{1,2,0:T(8,128)(2,1)S(1)}, bf16[2,256,512]{1,2,0:T(8,128)(2,1)}, u32[]{:S(2)}, u32[]{:S(2)}) collective-permute-start(bf16[2,256,512]{1,2,0:T(8,128)(2,1)S(1)} %copy.27), channel_id=1, source_target_pairs={{0,2},{2,4},{4,6},{6,8},{8,10},{10,12},{12,14},{14,16},{16,18},{18... | collective-permute-start | bytes 1572872 | tf_op jit(solution)/shard_map/ppermute | solution.py:22
  17.8 46.7 %collective-permute-start.4 = (bf16[2,256,512]{1,2,0:T(8,128)(2,1)S(1)}, bf16[2,256,512]{1,2,0:T(8,128)(2,1)}, u32[]{:S(2)}, u32[]{:S(2)}) collective-permute-start(bf16[2,256,512]{1,2,0:T(8,128)(2,1)S(1)} %copy.27), channel_id=1, source_target_pairs={{4,0},{6,2},{8,4},{10,6},{12,8},{14,10},{16,12},{18,14},{20,16},{2... | collective-permute-start | bytes 1572872 | tf_op jit(solution)/shard_map/ppermute | solution.py:22
  21.9 22.7 %collective-permute-start.6 = (s32[2,256]{1,0:T(2,128)S(1)}, s32[2,256]{1,0:T(2,128)S(1)}, u32[]{:S(2)}, u32[]{:S(2)}) collective-permute-start(s32[2,256]{1,0:T(2,128)S(1)} %copy-done.24), channel_id=1, source_target_pairs={{4,0},{6,2},{8,4},{10,6},{12,8},{14,10},{16,12},{18,14},{20,16},{2... | collective-permute-start | bytes 6152 | tf_op jit(solution)/shard_map/ppermute | solution.py:22
  26.6 13.4 %collective-permute-start.7 = (s32[2,256]{1,0:T(2,128)S(1)}, s32[2,256]{1,0:T(2,128)S(1)}, u32[]{:S(2)}, u32[]{:S(2)}) collective-permute-start(s32[2,256]{1,0:T(2,128)S(1)} %copy-done.24), channel_id=1, source_target_pairs={{2,0},{4,2},{6,4},{8,6},{10,8},{12,10},{14,12},{16,14},{18,16},{20... | collective-permute-start | bytes 6152 | tf_op jit(solution)/shard_map/ppermute | solution.py:22
  29.6 46.0 %copy-start.13 = (bf16[256,256]{0,1:T(8,128)(2,1)}, bf16[256,256]{0,1:T(8,128)(2,1)S(1)}, u32[]{:S(2)}) copy-start(bf16[256,256]{0,1:T(8,128)(2,1)S(1)} %get-tuple-element.44) | copy-start | bytes 393220
  40.0 10.4 %collective-permute-start.3 = (s32[2,256]{1,0:T(2,128)S(1)}, s32[2,256]{1,0:T(2,128)S(1)}, u32[]{:S(2)}, u32[]{:S(2)}) collective-permute-start(s32[2,256]{1,0:T(2,128)S(1)} %copy-done.24), channel_id=1, source_target_pairs={{0,2},{2,4},{4,6},{6,8},{8,10},{10,12},{12,14},{14,16},{16,18},{18... | collective-permute-start | bytes 6152 | tf_op jit(solution)/shard_map/ppermute | solution.py:22
  44.6 19.8 %collective-permute-start = (bf16[2,256,512]{1,2,0:T(8,128)(2,1)S(1)}, bf16[2,256,512]{1,2,0:T(8,128)(2,1)S(1)}, u32[]{:S(2)}, u32[]{:S(2)}) collective-permute-start(bf16[2,256,512]{1,2,0:T(8,128)(2,1)S(1)} %copy.27), channel_id=1, source_target_pairs={{0,4},{2,6},{4,8},{6,10},{8,12},{10,14},{12,16},{14,18},{16,20},{1... | collective-permute-start | bytes 1572872 | tf_op jit(solution)/shard_map/ppermute | solution.py:22
  50.4 11.0 %collective-permute-start.2 = (s32[2,256]{1,0:T(2,128)S(1)}, s32[2,256]{1,0:T(2,128)S(1)}, u32[]{:S(2)}, u32[]{:S(2)}) collective-permute-start(s32[2,256]{1,0:T(2,128)S(1)} %copy-done.24), channel_id=1, source_target_pairs={{0,4},{2,6},{4,8},{6,10},{8,12},{10,14},{12,16},{14,18},{16,20},{1... | collective-permute-start | bytes 6152 | tf_op jit(solution)/shard_map/ppermute | solution.py:22
  66.8 3.5 copy-start.17
  66.8 3.5 copy-start.21
  70.3 2.0 copy-start.2
  75.6 3.4 copy-start.20
  79.0 1.9 copy-start.4
  79.0 1.9 copy-start.19
  82.4 1.1 copy-start.10
  83.9 50.7 %collective-permute-start.11 = (f32[2,256,512]{1,2,0:T(8,128)S(1)}, f32[2,256,512]{1,2,0:T(8,128)S(1)}, u32[]{:S(2)}, u32[]{:S(2)}) collective-permute-start(f32[2,256,512]{1,2,0:T(8,128)S(1)} %stack.47), channel_id=1, source_target_pairs={{0,4},{2,6},{4,8},{6,10},{8,12},{10,14},{12,16},{14,18},{16,20},{1... | collective-permute-start | bytes 3145736 | tf_op jit(solution)/shard_map/ppermute | solution.py:22
  88.6 65.0 %collective-permute-start.10 = (f32[2,256,512]{1,2,0:T(8,128)S(1)}, f32[2,256,512]{1,2,0:T(8,128)S(1)}, u32[]{:S(2)}, u32[]{:S(2)}) collective-permute-start(f32[2,256,512]{1,2,0:T(8,128)S(1)} %pad_maximum_fusion), channel_id=1, source_target_pairs={{0,2},{2,4},{4,6},{6,8},{8,10},{10,12},{12,14},{14,16},{16,18},{18... | collective-permute-start | bytes 3145736 | tf_op jit(solution)/shard_map/ppermute | solution.py:22
  90.7 9.6 %copy-start.3 = (f32[2,256,768]{2,1,0:T(8,128)S(1)}, f32[2,256,768]{2,1,0:T(8,128)}, u32[]{:S(2)}) copy-start(f32[2,256,768]{2,1,0:T(8,128)} %get-tuple-element.53) | copy-start | bytes 4718596
  90.7 9.6 %copy-start.18 = (bf16[768,256]{0,1:T(8,128)(2,1)S(1)}, bf16[768,256]{0,1:T(8,128)(2,1)}, u32[]{:S(2)}) copy-start(bf16[768,256]{0,1:T(8,128)(2,1)} %get-tuple-element.37) | copy-start | bytes 1179652
  90.7 65.4 %collective-permute-start.9 = (f32[2,256,512]{1,2,0:T(8,128)S(1)}, f32[2,256,512]{1,2,0:T(8,128)S(1)}, u32[]{:S(2)}, u32[]{:S(2)}) collective-permute-start(f32[2,256,512]{1,2,0:T(8,128)S(1)} %stack.42), channel_id=1, source_target_pairs={{4,0},{6,2},{8,4},{10,6},{12,8},{14,10},{16,12},{18,14},{20,16},{2... | collective-permute-start | bytes 3145736 | tf_op jit(solution)/shard_map/ppermute | solution.py:22
  94.5 72.1 %collective-permute-start.8 = (f32[2,256,512]{1,2,0:T(8,128)S(1)}, f32[2,256,512]{1,2,0:T(8,128)S(1)}, u32[]{:S(2)}, u32[]{:S(2)}) collective-permute-start(f32[2,256,512]{1,2,0:T(8,128)S(1)} %stack.40), channel_id=1, source_target_pairs={{2,0},{4,2},{6,4},{8,6},{10,8},{12,10},{14,12},{16,14},{18,16},{20... | collective-permute-start | bytes 3145736 | tf_op jit(solution)/shard_map/ppermute | solution.py:22
  169.4 1.3 copy-start.5
  397.5 4.2 %copy-start.12 = (f32[512,256]{0,1:T(8,128)S(1)}, f32[512,256]{0,1:T(8,128)}, u32[]{:S(2)}) copy-start(f32[512,256]{0,1:T(8,128)} %get-tuple-element.20) | copy-start | bytes 1572868
  397.5 5.2 %copy-start.11 = (f32[256,512]{1,0:T(8,128)S(1)}, f32[256,512]{1,0:T(8,128)}, u32[]{:S(2)}) copy-start(f32[256,512]{1,0:T(8,128)} %get-tuple-element.69) | copy-start | bytes 1572868
  (7 other events, 6.4 us)
Sparse Core Ops, SparseCore 0:
  169.5 227.9 all-reduce.7
where the time goes:
time: 413 us; the launch traced here: 410 us
  waiting for transfers between devices  299 us (72%)
  starting transfers between devices  42.8 us (10%)
  matrix products  23.8 us (6%)
  between operations  14.7 us (4%)
  local copies, waits for them, and re-layouts  14.4 us (3%)
  blocking collectives  9.29 us (2%)
  other arithmetic  6.67 us (2%)
    psum x1, waiting for transfers between devices, shards(): lax.psum((term_query, term_key, term_value, term_out), 'tm')  216 us
    ppermute x12, waiting for transfers between devices, passed_along(): return lax.ppermute(block, axis, route)  82.4 us
    ppermute x12, starting transfers between devices, passed_along(): return lax.ppermute(block, axis, route)  42.7 us
    unnamed x56, local copies, waits for them, and re-layouts  9.6 us
    psum x1, blocking collectives, shards(): lax.psum(partial_out, 'rep').astype(jnp.bfloat16)  9.29 us
  transfers between devices with their start and end apart: 13, of which 8 were waited for; matrix products, arithmetic and copies ran while one was open for 3% of the time, Pallas kernels for 0%

commit v1 on v0

v1 whole, which is shorter than its diff:
```python
import functools
import math

import jax
import jax.numpy as jnp
from jax import lax
from jax.experimental import pallas as pl
from jax.experimental.pallas import tpu as pltpu
from jax.sharding import PartitionSpec as P

HD = 128
BLK = 256
WIN = 3 * BLK
D = 512
NX, NY, NZ = 4, 4, 8
LOG2E = 1.4426950408889634
MESH = pl.DeviceIdType.MESH
F32 = jnp.float32
BF16 = jnp.bfloat16
ORDERS = (("x", "y", "z"), ("y", "x", "z"))
SIZES = {"x": NX, "y": NY, "z": NZ}


def nt(a, b):
    return lax.dot_general(a, b, (((1,), (1,)), ((), ())), preferred_element_type=F32)


def nn(a, b):
    return jnp.dot(a, b, preferred_element_type=F32)


def kernel(
    tm_size,
    table,
    cot,
    stamps,
    starts,
    wq_in,
    wk_in,
    wv_in,
    wo_in,
    decay,
    mixed_out,
    gt_out,
    red_out,
    xw,
    xT,
    g_s,
    ts_near,
    dec_send,
    dec_recv,
    wq,
    wk,
    wv,
    wo,
    mb,
    brow,
    q_s,
    qT_s,
    k_s,
    v_s,
    do_s,
    doT_s,
    o_s,
    dq_s,
    dkT_s,
    dvT_s,
    pf,
    psend,
    precv,
    b0,
    b1,
    b2,
    rc0,
    rc1,
    rc2,
    red,
    ct_send,
    ct_recv,
    ct_own,
    mix,
    gtb,
    lsem,
    osem,
    hs,
    hr,
    ws,
    wr,
    ps,
    pr,
    rs_s,
    rs_r,
    ag_s,
    ag_r,
    cs,
    cr,
    ms,
    mr,
):
    tm = lax.axis_index("tm")
    c = lax.axis_index("rep")
    blocks = 2 * tm_size
    blk = c * (blocks - 1 - 2 * tm) + tm
    coord = {"x": tm // (NZ * NY), "z": (tm // NY) % NZ, "y": tm % NY}

    def holder(pos):
        side = pos // tm_size
        return (side * (blocks - 1 - 2 * pos) + pos, side)

    def partner(axis, d):
        at = dict(coord)
        at[axis] = (coord[axis] + d) % SIZES[axis]
        return ((at["x"] * NZ + at["z"]) * NY + at["y"], c)

    next1 = holder((blk + 1) % blocks)
    next2 = holder((blk + 2) % blocks)
    pos1 = (blk + blocks - 1) % blocks
    pos2 = (blk + blocks - 2) % blocks
    prev1 = holder(pos1)
    prev2 = holder(pos2)
    sib = (tm, 1 - c)

    loads = [
        pltpu.make_async_copy(src, dst, lsem.at[n])
        for n, (src, dst) in enumerate(
            [
                (table.at[c], xw.at[2]),
                (cot.at[c], g_s),
                (wq_in, wq.at[1]),
                (wk_in, wk.at[1]),
                (wv_in, wv.at[1]),
                (wo_in, wo.at[1]),
            ]
        )
    ]
    for copy in loads:
        copy.start()

    barrier = pltpu.get_barrier_semaphore()
    friends = [next1, next2, prev1, prev2, sib]
    for axis, size in SIZES.items():
        friends += [partner(axis, d) for d in range(1, size)]
    for friend in friends:
        pl.semaphore_signal(barrier, inc=1, device_id=friend, device_id_type=MESH)

    def remote(src, dst, send, recv, to):
        return pltpu.make_async_remote_copy(
            src_ref=src, dst_ref=dst, send_sem=send, recv_sem=recv, device_id=to, device_id_type=MESH
        )

    sub = lax.broadcasted_iota(jnp.int32, (8, 128), 0)
    dec_send[...] = jnp.where(sub == 0, decay[0, 0], decay[0, 1])
    first_row = jnp.where(c == 0, starts[0:1, :], starts[1:2, :]) - (blk - 2) * BLK
    first_col = jnp.transpose(jnp.broadcast_to(first_row.astype(F32), (128, BLK)))
    row_id = lax.broadcasted_iota(jnp.int32, (BLK, 128), 0)
    col_id = lax.broadcasted_iota(jnp.int32, (BLK, 128), 1)
    for n in range(WIN // 128):
        key_id = col_id + n * 128
        ok = (key_id.astype(F32) >= first_col) & (key_id <= row_id + 2 * BLK)
        mb[:, n * 128 : (n + 1) * 128] = jnp.where(ok, 0.0, -1e30)

    pl.semaphore_wait(barrier, len(friends))

    half = BLK // 2
    top, low = pl.ds(0, half), pl.ds(half, half)
    mine = [
        remote(table.at[c, rows], xw.at[1, rows], hs.at[n], hr.at[n], next1)
        for n, rows in enumerate((top, low))
    ]
    onward = [
        remote(xw.at[1, rows], xw.at[0, rows], hs.at[2 + n], hr.at[2 + n], next1)
        for n, rows in enumerate((top, low))
    ]
    times = [
        remote(stamps, ts_near.at[n], hs.at[4 + n], hr.at[4 + n], to)
        for n, to in enumerate((next1, next2))
    ]
    weights = [
        remote(src, dst.at[0], ws.at[n], wr.at[n], sib)
        for n, (src, dst) in enumerate(((wq_in, wq), (wk_in, wk), (wv_in, wv), (wo_in, wo)))
    ]
    decays = remote(dec_send, dec_recv, ws.at[4], wr.at[4], sib)
    for copy in mine + times + [decays] + weights:
        copy.start()

    def put_heads(dst, slot, rows, val):
        val = val.astype(BF16)
        for j in range(2):
            dst[2 * j + slot, rows, :] = val[:, j * HD : (j + 1) * HD]
        return val

    every = pl.ds(0, BLK)

    def own_rows(slot):
        x = xw[2]
        val = put_heads(q_s, slot, every, nn(x, wq[slot]))
        for j in range(2):
            qT_s[2 * j + slot] = jnp.transpose(val[:, j * HD : (j + 1) * HD])
        val = put_heads(do_s, slot, every, nt(g_s[...], wo[slot]))
        for j in range(2):
            doT_s[2 * j + slot] = jnp.transpose(val[:, j * HD : (j + 1) * HD])

    def keys_of(part, slot):
        rows = pl.ds(part * BLK, BLK)
        put_heads(k_s, slot, rows, nn(xw[part], wk[slot]))
        put_heads(v_s, slot, rows, nn(xw[part], wv[slot]))

    for copy in loads:
        copy.wait()
    own_rows(1)
    keys_of(2, 1)
    xT[:, 2 * BLK :] = jnp.transpose(xw[2])
    for n in range(2):
        mine[n].wait_recv()
        onward[n].start()
    keys_of(1, 1)
    xT[:, BLK : 2 * BLK] = jnp.transpose(xw[1])
    for copy in weights:
        copy.wait_recv()
    own_rows(0)
    keys_of(2, 0)
    keys_of(1, 0)
    for copy in times + [decays]:
        copy.wait_recv()
    for copy in onward:
        copy.wait_recv()
    keys_of(0, 0)
    keys_of(0, 1)
    xT[:, :BLK] = jnp.transpose(xw[0])

    def side_row(ref, pos):
        return jnp.where(pos // tm_size == 0, ref[0:1, :], ref[1:2, :])

    own_times = side_row(stamps, blk)
    base = jnp.max(own_times, axis=1, keepdims=True)
    rel = jnp.concatenate(
        [side_row(ts_near.at[1], pos2), side_row(ts_near.at[0], pos1), own_times], axis=1
    )
    rel = (rel - base).astype(F32) * LOG2E
    for j in range(2):
        brow[2 * j] = rel * dec_recv[j : j + 1, 0:1]
        brow[2 * j + 1] = rel * dec_send[j : j + 1, 0:1]

    inv_scale = 1.0 / math.sqrt(HD)
    psends = [
        remote(psend.at[j], precv.at[j], ps.at[j], pr.at[j], sib) for j in range(2)
    ]

    def head(t, carry):
        slot = t % 2
        j = t // 2
        lanes = pl.ds(pl.multiple_of(j * HD, HD), HD)
        s = nt(q_s[t], k_s[t]) * (inv_scale * LOG2E) + (mb[...] + brow[t])
        p = jnp.exp2(s - jnp.max(s, axis=-1, keepdims=True))
        p = p * (1.0 / jnp.sum(p, axis=-1, keepdims=True))
        pb = p.astype(BF16)
        o = nn(pb, v_s[t]).astype(BF16)
        o_s[slot, :, lanes] = o
        dvT = nn(doT_s[t], pb).astype(BF16)
        dvT_s[slot, j] = dvT
        dp = nt(do_s[t], v_s[t])
        delta = jnp.sum(p * dp, axis=-1, keepdims=True)
        ds = (p * (dp - delta)).astype(BF16)
        dq = (nn(ds, k_s[t]) * inv_scale).astype(BF16)
        dq_s[slot, :, lanes] = dq
        dkT = (nn(qT_s[t], ds) * inv_scale).astype(BF16)
        dkT_s[slot, j] = dkT
        pf[0:D, :] = nn(xT[:, 2 * BLK :], dq)
        pf[D : 2 * D, :] = nt(xT[...], dkT)
        pf[2 * D : 3 * D, :] = nt(xT[...], dvT)
        go = nn(jnp.transpose(o), g_s[...])
        for n in range(4):
            pf[3 * D + n * HD : 3 * D + (n + 1) * HD, :] = go[:, n * HD : (n + 1) * HD]

        for jj in range(2):

            @pl.when(t == 2 * jj)
            def _():
                psend[jj] = pf[...].astype(BF16)
                psends[jj].start()

            @pl.when(t == 2 * jj + 1)
            def _():
                psends[jj].wait_recv()
                for n in range(4):
                    total = pf[n * D : (n + 1) * D, :] + precv[jj, n * D : (n + 1) * D, :].astype(F32)
                    at = ((n % 2) * 2 + jj) * D
                    b0[n // 2, at : at + D, :] = total.astype(BF16)

        return carry

    lax.fori_loop(0, 4, head, 0)

    sources = (b0, b1, b2)
    landing = (rc0, rc1, rc2)
    rows_at = (4 * D, D, D // 4)

    def scatter(stage):
        copies = []
        for col in range(2):
            axis = ORDERS[col][stage]
            size = SIZES[axis]
            piece = rows_at[stage] // size
            for d in range(1, size):
                there = (coord[axis] + d) % size
                copies.append(
                    remote(
                        sources[stage].at[col, pl.ds(pl.multiple_of(there * piece, piece), piece)],
                        landing[stage].at[col, d - 1],
                        rs_s.at[stage, col, d - 1],
                        rs_r.at[stage, col, d - 1],
                        partner(axis, d),
                    )
                )
        for copy in copies:
            copy.start()
        return copies

    def gathered(stage, col):
        axis = ORDERS[col][stage]
        size = SIZES[axis]
        piece = rows_at[stage] // size
        own = sources[stage][col, pl.ds(pl.multiple_of(coord[axis] * piece, piece), piece), :]
        total = own.astype(F32)
        for d in range(1, size):
            total = total + landing[stage][col, d - 1].astype(F32)
        return total

    def base_row(stage, col):
        row = 0
        for s in range(stage + 1):
            axis = ORDERS[col][s]
            row = row + coord[axis] * (rows_at[s] // SIZES[axis])
        return row

    def spread(stage):
        copies = []
        for col in range(2):
            axis = ORDERS[col][stage]
            size = SIZES[axis]
            piece = rows_at[stage] // size
            here = pl.ds(pl.multiple_of(base_row(stage, col), piece), piece)
            for d in range(1, size):
                copies.append(
                    remote(
                        red.at[col, here],
                        red.at[col, here],
                        ag_s.at[stage, col, d - 1],
                        ag_r.at[stage, col, d - 1],
                        partner(axis, d),
                    )
                )
        for copy in copies:
            copy.start()
        return copies

    def arrived(copies):
        for copy in copies:
            copy.wait_recv()

    sent = []
    first = scatter(0)
    sent += first

    mix[c] = (nn(o_s[0], wo[0]) + nn(o_s[1], wo[1])).astype(BF16)
    to_sib = [remote(mix.at[c], mix.at[c], ms.at[0], mr.at[0], sib)]
    to_sib[0].start()
    for part in range(3):
        cols = slice(part * BLK, (part + 1) * BLK)
        total = jnp.zeros((D, BLK), F32)
        for slot in range(2):
            total = total + nn(wk[slot], dkT_s[slot, :, :, cols].reshape(BLK, BLK))
            total = total + nn(wv[slot], dvT_s[slot, :, :, cols].reshape(BLK, BLK))
        if part == 2:
            ct_own[...] = total
        else:
            ct_send[part] = total.astype(BF16)
    terms = [
        remote(ct_send.at[n], ct_recv.at[n], cs.at[n], cr.at[n], to)
        for n, to in enumerate((prev2, prev1))
    ]

    arrived(first)
    for col in range(2):
        b1[col] = gathered(0, col).astype(BF16)
    second = scatter(1)
    sent += second
    for copy in terms:
        copy.start()
    gtq = nt(dq_s[0], wq[0]) + nt(dq_s[1], wq[1])
    arrived(second)
    for col in range(2):
        b2[col] = gathered(1, col).astype(BF16)
    third = scatter(2)
    sent += third
    arrived(third)
    scale = 1.0 / math.sqrt(blocks * BLK)
    for col in range(2):
        piece = rows_at[2] // NZ
        here = pl.ds(pl.multiple_of(base_row(2, col), piece), piece)
        red[col, here, :] = (gathered(2, col) * scale).astype(BF16)
    up = spread(2)
    sent += up
    for copy in terms:
        copy.wait_recv()
    ct = ct_own[...] + ct_recv[0].astype(F32) + ct_recv[1].astype(F32)
    gtb[c] = (gtq + jnp.transpose(ct)).astype(BF16)
    to_sib.append(remote(gtb.at[c], gtb.at[c], ms.at[1], mr.at[1], sib))
    to_sib[1].start()
    arrived(up)
    up = spread(1)
    sent += up
    arrived(up)
    up = spread(0)
    sent += up
    arrived(to_sib)
    outs = [
        pltpu.make_async_copy(mix, mixed_out, osem.at[0]),
        pltpu.make_async_copy(gtb, gt_out, osem.at[1]),
    ]
    for copy in outs:
        copy.start()
    arrived(up)
    outs.append(pltpu.make_async_copy(red, red_out, osem.at[2]))
    outs[2].start()
    for copy in mine + onward + times + [decays] + weights + psends + sent + terms + to_sib:
        copy.wait_send()
    for copy in outs:
        copy.wait()


def shards(table, cotangent, stamps, starts, w_query, w_key, w_value, w_out, decay):
    tm_size = lax.axis_size("tm")
    hbm = pl.BlockSpec(memory_space=pl.ANY)
    vmem = pl.BlockSpec(memory_space=pltpu.VMEM)
    dma = pltpu.SemaphoreType.DMA
    V = pltpu.VMEM
    mixed, grad_table, red = pl.pallas_call(
        functools.partial(kernel, tm_size),
        out_shape=(
            jax.ShapeDtypeStruct((2, BLK, D), BF16),
            jax.ShapeDtypeStruct((2, BLK, D), BF16),
            jax.ShapeDtypeStruct((2, 4 * D, 128), BF16),
        ),
        in_specs=[hbm, hbm, vmem, vmem, hbm, hbm, hbm, hbm, pl.BlockSpec(memory_space=pltpu.SMEM)],
        out_specs=(hbm, hbm, hbm),
        scratch_shapes=[
            V((3, BLK, D), BF16),
            V((D, WIN), BF16),
            V((BLK, D), BF16),
            V((2, 2, BLK), jnp.int32),
            V((8, 128), F32),
            V((8, 128), F32),
            V((2, D, BLK), BF16),
            V((2, D, BLK), BF16),
            V((2, D, BLK), BF16),
            V((2, BLK, D), BF16),
            V((BLK, WIN), F32),
            V((4, 1, WIN), F32),
            V((4, BLK, HD), BF16),
            V((4, HD, BLK), BF16),
            V((4, WIN, HD), BF16),
            V((4, WIN, HD), BF16),
            V((4, BLK, HD), BF16),
            V((4, HD, BLK), BF16),
            V((2, BLK, BLK), BF16),
            V((2, BLK, BLK), BF16),
            V((2, 2, HD, WIN), BF16),
            V((2, 2, HD, WIN), BF16),
            V((4 * D, 128), F32),
            V((2, 4 * D, 128), BF16),
            V((2, 4 * D, 128), BF16),
            V((2, 4 * D, 128), BF16),
            V((2, D, 128), BF16),
            V((2, D // 4, 128), BF16),
            V((2, 3, D, 128), BF16),
            V((2, 3, D // 4, 128), BF16),
            V((2, 7, D // 32, 128), BF16),
            V((2, 4 * D, 128), BF16),
            V((2, D, BLK), BF16),
            V((2, D, BLK), BF16),
            V((D, BLK), F32),
            V((2, BLK, D), BF16),
            V((2, BLK, D), BF16),
            dma((6,)),
            dma((3,)),
            dma((6,)),
            dma((6,)),
            dma((5,)),
            dma((5,)),
            dma((2,)),
            dma((2,)),
            dma((3, 2, 7)),
            dma((3, 2, 7)),
            dma((3, 2, 7)),
            dma((3, 2, 7)),
            dma((2,)),
            dma((2,)),
            dma((2,)),
            dma((2,)),
        ],
        compiler_params=pltpu.CompilerParams(
            collective_id=0, has_side_effects=True, vmem_limit_bytes=56 * 1024 * 1024
        ),
        name="history_attention",
    )(table, cotangent, stamps, starts, w_query, w_key, w_value, w_out, decay.reshape(1, 2))
    red = red.reshape(4, 2, D, 128).astype(F32)

    def wide(part):
        return jnp.transpose(part, (1, 0, 2)).reshape(D, 256)

    grad_out = jnp.transpose(red[3].reshape(2, 4, 128, 128), (0, 2, 1, 3)).reshape(256, D)
    return (mixed, grad_table, wide(red[0]), wide(red[1]), wide(red[2]), grad_out)


def solution(mesh):
    return jax.shard_map(
        shards,
        mesh=mesh,
        in_specs=(
            P(None, "tm", None),
            P(None, "tm", None),
            P(None, "tm"),
            P(None, "tm"),
            P(None, "rep"),
            P(None, "rep"),
            P(None, "rep"),
            P("rep", None),
            P("rep"),
        ),
        out_specs=(
            P(None, "tm", None),
            P(None, "tm", None),
            P(None, "rep"),
            P(None, "rep"),
            P(None, "rep"),
            P("rep", None),
        ),
        check_vma=False,
    )
```

time: 413 us -> 79 us (0.19)
  waiting for transfers between devices: 299 us -> 0 us
  Pallas kernels: 0 us -> 72.2 us
  starting transfers between devices: 42.8 us -> 0 us
  matrix products: 23.8 us -> 0 us
  between operations: 14.7 us -> 0.69 us
  blocking collectives: 9.29 us -> 0 us
  local copies, waits for them, and re-layouts: 14.4 us -> 5.83 us
  other arithmetic: 6.67 us -> 0.14 us
    psum x1 -> x0, waiting for transfers between devices: 216 us -> none  [shards(): lax.psum((term_query, term_key, term_value, term_out), 'tm')]
    ppermute x12 -> x0, waiting for transfers between devices: 82.4 us -> none  [passed_along(): return lax.ppermute(block, axis, route)]
    pallas_call x0 -> x1, Pallas kernels: none -> 72.2 us  [shards(): pl.pallas_call(functools.partial(kernel, tm_size), out_shape=(jax.ShapeDt...]
    ppermute x12 -> x0, starting transfers between devices: 42.7 us -> none  [passed_along(): return lax.ppermute(block, axis, route)]
    dot_general x22 -> x0, matrix products: 17 us -> none  [the longest x2 3.15 us: attend(): jnp.einsum('hqk,qhd->khd', probs_low, g_heads, preferred_element_type=jnp...]
    psum x1 -> x0, blocking collectives: 9.29 us -> none  [shards(): lax.psum(partial_out, 'rep').astype(jnp.bfloat16)]
    unnamed x56 -> x10, local copies, waits for them, and re-layouts: 9.6 us -> 2.53 us
    sub x2 -> x0, matrix products: 6.86 us -> none  [attend(): weights = jnp.where(allowed[None], jnp.exp(scores - row_max), 0.0)]
  transfers between devices with their start and end apart: 13 -> 0, of which waited for: 8 -> 0; matrix products, arithmetic and copies ran while one was open for 3% -> 0% of each run, Pallas kernels for 0% -> 0%
where the time goes in v1:
time: 79 us; the launch traced here: 78.8 us
  Pallas kernels  72.2 us (91%)
  local copies, waits for them, and re-layouts  5.83 us (7%)
    pallas_call x1, Pallas kernels, shards(): pl.pallas_call(functools.partial(kernel, tm_size), out_shape=(jax.ShapeDt...  72.2 us
    unnamed x10, local copies, waits for them, and re-layouts  2.53 us
    reshape x2, local copies, waits for them, and re-layouts, wide(): return jnp.transpose(part, (1, 0, 2)).reshape(D, 256)  1.88 us

profile of v1, /device:TPU:32, one launch (start us, length us, event | category | flops | bytes accessed | tf_op | source)
XLA Modules:
  0.0 78.8 jit_solution(15012209683845759014)
XLA Ops:
  0.6 72.2 %history_attention.1 = (bf16[2,256,512]{2,1,0:T(8,128)(2,1)}, bf16[2,256,512]{2,1,0:T(8,128)(2,1)}, bf16[2,2048,128]{2,1,0:T(8,128)(2,1)}) custom-call(bf16[2,256,512]{2,1,0:T(8,128)(2,1)} %table.1, bf16[2,256,512]{2,1,0:T(8,128)(2,1)} %cot.1, s32[2,256]{1,0:T(2,128)} %stamps.1, s32[2,256]{1,0:T(2,128)} %starts.1, bf16[512,256]{1,0:T(8,128)(2,1)} %wq_in.1, ...), custom_call_target="tpu_custom_call" | custom-call | tf_op jit(solution)/shard_map/history_attention/pallas_call | solution.py:438
  72.8 0.0 copy-start
  72.8 1.1 %slice.19 = f32[1,2,512,128]{3,2,1,0:T(8,128)S(1)} slice(bf16[4,2,512,128]{3,2,1,0:T(8,128)(2,1)} %bitcast.32), slice={[3:4], [0:2], [0:512], [0:128]} | slice | bytes 1048576 | tf_op jit(solution)/shard_map/slice | solution.py:512
  73.9 0.3 copy.18
  74.2 0.8 %copy.27 = f32[32,8,4,128]{3,1,2,0:T(8,128)} copy(f32[32,8,4,128]{3,2,1,0:T(4,128)S(1)} %bitcast.34) | data formatting | bytes 1048576
  75.1 0.0 copy-done
  75.1 0.1 convert.1
  75.2 0.1 slice_bitcast_fusion
  75.3 0.0 copy-start.2
  75.3 0.0 copy-start.1
  75.3 1.0 %copy_bitcast_fusion.1 = (f32[512,256]{1,0:T(8,128)}, f32[512,256]{1,0:T(8,128)}) fusion(f32[2,64,8,128]{3,2,1,0:T(8,128)S(1)} %get-tuple-element.12, f32[2,64,8,128]{3,2,1,0:T(8,128)S(1)} %get-tuple-element.13), kind=kLoop, calls=%fused_computation.1 | loop fusion | bytes 2097152 | tf_op jit(solution)/shard_map/reshape | solution.py:510
  76.4 0.8 %copy.28 = f32[2,64,8,128]{3,2,0,1:T(8,128)} copy(f32[2,64,8,128]{3,2,1,0:T(8,128)S(1)} %get-tuple-element.14) | data formatting | bytes 1048576 | tf_op jit(solution)/shard_map/reshape | solution.py:510
  77.2 0.0 copy-done.2
  77.2 0.8 %copy.31 = bf16[2,256,512]{2,1,0:T(8,128)(2,1)} copy(bf16[2,256,512]{2,1,0:T(8,128)(2,1)S(1)} %copy-done.2) | data formatting | bytes 1048576
  78.0 0.0 copy-done.1
  78.0 0.8 %copy.32 = bf16[2,256,512]{2,1,0:T(8,128)(2,1)} copy(bf16[2,256,512]{2,1,0:T(8,128)(2,1)S(1)} %copy-done.1) | data formatting | bytes 1048576
Async XLA Ops:
  72.8 2.3 %copy-start = (bf16[2,2048,128]{2,1,0:T(8,128)(2,1)S(1)}, bf16[2,2048,128]{2,1,0:T(8,128)(2,1)}, u32[]{:S(2)}) copy-start(bf16[2,2048,128]{2,1,0:T(8,128)(2,1)} %get-tuple-element.11) | copy-start | bytes 3145732
  75.3 1.9 %copy-start.2 = (bf16[2,256,512]{2,1,0:T(8,128)(2,1)S(1)}, bf16[2,256,512]{2,1,0:T(8,128)(2,1)}, u32[]{:S(2)}) copy-start(bf16[2,256,512]{2,1,0:T(8,128)(2,1)} %get-tuple-element.23) | copy-start | bytes 1572868
  75.3 2.7 %copy-start.1 = (bf16[2,256,512]{2,1,0:T(8,128)(2,1)S(1)}, bf16[2,256,512]{2,1,0:T(8,128)(2,1)}, u32[]{:S(2)}) copy-start(bf16[2,256,512]{2,1,0:T(8,128)(2,1)} %get-tuple-element.24) | copy-start | bytes 1572868

commit v2 on v1

v2 whole, which is shorter than its diff:
```python
import functools
import math

import jax
import jax.numpy as jnp
from jax import lax
from jax.experimental import pallas as pl
from jax.experimental.pallas import tpu as pltpu
from jax.sharding import PartitionSpec as P

HD = 128
BLK = 256
WIN = 3 * BLK
D = 512
NX, NY, NZ = 4, 4, 8
LOG2E = 1.4426950408889634
MESH = pl.DeviceIdType.MESH
F32 = jnp.float32
BF16 = jnp.bfloat16
ORDERS = (("x", "y", "z"), ("y", "x", "z"))
SIZES = {"x": NX, "y": NY, "z": NZ}


def nt(a, b):
    return lax.dot_general(a, b, (((1,), (1,)), ((), ())), preferred_element_type=F32)


def nn(a, b):
    return jnp.dot(a, b, preferred_element_type=F32)


def kernel(
    tm_size,
    table,
    cot,
    stamps,
    starts,
    wq_in,
    wk_in,
    wv_in,
    wo_in,
    decay,
    mix,
    gtb,
    red,
    xw,
    xT,
    g_s,
    ts_own,
    st_own,
    dec_in,
    ts_near,
    dec_send,
    dec_recv,
    wq,
    wk,
    wv,
    wo,
    mb,
    brow,
    q_s,
    qT_s,
    k_s,
    v_s,
    do_s,
    doT_s,
    o_s,
    dq_s,
    dkT_s,
    dvT_s,
    psend,
    precv,
    pown,
    b0,
    b1,
    b2,
    rc0,
    rc1,
    rc2,
    ct_send,
    ct_recv,
    ct_own,
    lsem,
    hs,
    hr,
    ws,
    wr,
    ps,
    pr,
    rs_s,
    rs_r,
    ag_s,
    ag_r,
    cs,
    cr,
    ms,
    mr,
):
    tm = lax.axis_index("tm")
    c = lax.axis_index("rep")
    blocks = 2 * tm_size
    blk = c * (blocks - 1 - 2 * tm) + tm
    coord = {"x": tm // (NZ * NY), "z": (tm // NY) % NZ, "y": tm % NY}

    def holder(pos):
        side = pos // tm_size
        return (side * (blocks - 1 - 2 * pos) + pos, side)

    def partner(axis, d):
        at = dict(coord)
        at[axis] = (coord[axis] + d) % SIZES[axis]
        return ((at["x"] * NZ + at["z"]) * NY + at["y"], c)

    next1 = holder((blk + 1) % blocks)
    next2 = holder((blk + 2) % blocks)
    pos1 = (blk + blocks - 1) % blocks
    pos2 = (blk + blocks - 2) % blocks
    prev1 = holder(pos1)
    prev2 = holder(pos2)
    sib = (tm, 1 - c)

    barrier = pltpu.get_barrier_semaphore()
    friends = [next1, next2, prev1, prev2, sib]
    for axis, size in SIZES.items():
        friends += [partner(axis, d) for d in range(1, size)]
    for friend in friends:
        pl.semaphore_signal(barrier, inc=1, device_id=friend, device_id_type=MESH)

    loads = [
        pltpu.make_async_copy(src, dst, lsem.at[n])
        for n, (src, dst) in enumerate(
            [
                (stamps, ts_own),
                (starts, st_own),
                (decay, dec_in),
                (table.at[c], xw.at[2]),
                (cot.at[c], g_s),
                (wq_in, wq.at[1]),
                (wk_in, wk.at[1]),
                (wv_in, wv.at[1]),
                (wo_in, wo.at[1]),
            ]
        )
    ]
    for copy in loads:
        copy.start()

    def remote(src, dst, send, recv, to):
        return pltpu.make_async_remote_copy(
            src_ref=src, dst_ref=dst, send_sem=send, recv_sem=recv, device_id=to, device_id_type=MESH
        )

    for copy in loads[:3]:
        copy.wait()
    sub = lax.broadcasted_iota(jnp.int32, (8, 128), 0)
    dec_send[...] = jnp.where(sub == 0, dec_in[0, 0], dec_in[0, 1])
    first_row = jnp.where(c == 0, st_own[0:1, :], st_own[1:2, :]) - (blk - 2) * BLK
    first_col = jnp.transpose(jnp.broadcast_to(first_row.astype(F32), (128, BLK)))
    row_id = lax.broadcasted_iota(jnp.int32, (BLK, 128), 0)
    col_id = lax.broadcasted_iota(jnp.int32, (BLK, 128), 1)
    for n in range(WIN // 128):
        key_id = col_id + n * 128
        ok = (key_id.astype(F32) >= first_col) & (key_id <= row_id + 2 * BLK)
        mb[:, n * 128 : (n + 1) * 128] = jnp.where(ok, 0.0, -1e30)

    pl.semaphore_wait(barrier, len(friends))

    half = BLK // 2
    top, low = pl.ds(0, half), pl.ds(half, half)
    mine = [
        remote(table.at[c, rows], xw.at[1, rows], hs.at[n], hr.at[n], next1)
        for n, rows in enumerate((top, low))
    ]
    onward = [
        remote(xw.at[1, rows], xw.at[0, rows], hs.at[2 + n], hr.at[2 + n], next1)
        for n, rows in enumerate((top, low))
    ]
    times = [
        remote(stamps, ts_near.at[n], hs.at[4 + n], hr.at[4 + n], to)
        for n, to in enumerate((next1, next2))
    ]
    weights = [
        remote(src, dst.at[0], ws.at[n], wr.at[n], sib)
        for n, (src, dst) in enumerate(((wq_in, wq), (wk_in, wk), (wv_in, wv), (wo_in, wo)))
    ]
    decays = remote(dec_send, dec_recv, ws.at[4], wr.at[4], sib)
    for copy in mine + times + [decays] + weights:
        copy.start()

    def put_heads(dst, slot, rows, val):
        val = val.astype(BF16)
        for j in range(2):
            dst[2 * j + slot, rows, :] = val[:, j * HD : (j + 1) * HD]
        return val

    every = pl.ds(0, BLK)

    def own_rows(slot):
        x = xw[2]
        val = put_heads(q_s, slot, every, nn(x, wq[slot]))
        for j in range(2):
            qT_s[2 * j + slot] = jnp.transpose(val[:, j * HD : (j + 1) * HD])
        val = put_heads(do_s, slot, every, nt(g_s[...], wo[slot]))
        for j in range(2):
            doT_s[2 * j + slot] = jnp.transpose(val[:, j * HD : (j + 1) * HD])

    def keys_of(part, slot):
        rows = pl.ds(part * BLK, BLK)
        put_heads(k_s, slot, rows, nn(xw[part], wk[slot]))
        put_heads(v_s, slot, rows, nn(xw[part], wv[slot]))

    for copy in loads[3:]:
        copy.wait()
    own_rows(1)
    keys_of(2, 1)
    xT[:, 2 * BLK :] = jnp.transpose(xw[2])
    for n in range(2):
        mine[n].wait_recv()
        onward[n].start()
    keys_of(1, 1)
    xT[:, BLK : 2 * BLK] = jnp.transpose(xw[1])
    for copy in weights:
        copy.wait_recv()
    own_rows(0)
    keys_of(2, 0)
    keys_of(1, 0)
    for copy in times + [decays]:
        copy.wait_recv()
    for copy in onward:
        copy.wait_recv()
    keys_of(0, 0)
    keys_of(0, 1)
    xT[:, :BLK] = jnp.transpose(xw[0])

    def side_row(ref, pos):
        return jnp.where(pos // tm_size == 0, ref[0:1, :], ref[1:2, :])

    own_times = side_row(ts_own, blk)
    base = jnp.max(own_times, axis=1, keepdims=True)
    rel = jnp.concatenate(
        [side_row(ts_near.at[1], pos2), side_row(ts_near.at[0], pos1), own_times], axis=1
    )
    rel = (rel - base).astype(F32) * LOG2E
    for j in range(2):
        brow[2 * j] = rel * dec_recv[j : j + 1, 0:1]
        brow[2 * j + 1] = rel * dec_send[j : j + 1, 0:1]

    inv_scale = 1.0 / math.sqrt(HD)
    psends = [
        remote(psend.at[j], precv.at[j], ps.at[j], pr.at[j], sib) for j in range(2)
    ]

    def head(t, carry):
        slot = t % 2
        j = t // 2
        lanes = pl.ds(pl.multiple_of(j * HD, HD), HD)
        s = nt(q_s[t], k_s[t]) * (inv_scale * LOG2E) + (mb[...] + brow[t])
        p = jnp.exp2(s - jnp.max(s, axis=-1, keepdims=True))
        p = p * (1.0 / jnp.sum(p, axis=-1, keepdims=True))
        pb = p.astype(BF16)
        o = nn(pb, v_s[t]).astype(BF16)
        o_s[slot, :, lanes] = o
        dvT = nn(doT_s[t], pb).astype(BF16)
        dvT_s[slot, j] = dvT
        dp = nt(do_s[t], v_s[t])
        delta = jnp.sum(p * dp, axis=-1, keepdims=True)
        ds = (p * (dp - delta)).astype(BF16)
        dq = (nn(ds, k_s[t]) * inv_scale).astype(BF16)
        dq_s[slot, :, lanes] = dq
        dkT = (nn(qT_s[t], ds) * inv_scale).astype(BF16)
        dkT_s[slot, j] = dkT
        parts = [
            nn(xT[:, 2 * BLK :], dq),
            nt(xT[...], dkT),
            nt(xT[...], dvT),
        ]
        go = nn(jnp.transpose(o), g_s[...])
        for n in range(3):
            pown[n] = parts[n]
        for n in range(4):
            pown[3, n * HD : (n + 1) * HD, :] = go[:, n * HD : (n + 1) * HD]

        for jj in range(2):

            @pl.when(t == 2 * jj)
            def _():
                psend[jj] = pown[...]
                psends[jj].start()

            @pl.when(t == 2 * jj + 1)
            def _():
                psends[jj].wait_recv()
                for n in range(4):
                    b0[jj, n // 2, (n % 2) * D : (n % 2 + 1) * D, :] = (pown[n] + precv[jj, n]).astype(BF16)
                for copy in scatters[jj][0]:
                    copy.start()

        return carry

    sources = (b0, b1, b2)
    landing = (rc0, rc1, rc2)
    rows_at = (2 * D, D // 2, D // 8)

    def place(stage, col):
        axis = ORDERS[col][stage]
        return axis, SIZES[axis], rows_at[stage] // SIZES[axis]

    def scatter(j, stage):
        copies = []
        for col in range(2):
            axis, size, piece = place(stage, col)
            for d in range(1, size):
                there = (coord[axis] + d) % size
                copies.append(
                    remote(
                        sources[stage].at[j, col, pl.ds(pl.multiple_of(there * piece, piece), piece)],
                        landing[stage].at[j, col, d - 1],
                        rs_s.at[j, stage, col, d - 1],
                        rs_r.at[j, stage, col, d - 1],
                        partner(axis, d),
                    )
                )
        return copies

    def gathered(j, stage, col):
        axis, size, piece = place(stage, col)
        total = sources[stage][j, col, pl.ds(pl.multiple_of(coord[axis] * piece, piece), piece), :].astype(F32)
        for d in range(1, size):
            total = total + landing[stage][j, col, d - 1].astype(F32)
        return total

    def first_owner(stage, col):
        owner = 0
        for s in range(stage + 1):
            axis, _, piece = place(s, col)
            owner = owner + coord[axis] * (piece // 8)
        return owner

    def spread(j, stage):
        copies = []
        for col in range(2):
            axis, size, piece = place(stage, col)
            here = pl.ds(first_owner(stage, col), piece // 8)
            for d in range(1, size):
                copies.append(
                    remote(
                        red.at[col, j, here],
                        red.at[col, j, here],
                        ag_s.at[j, stage, col, d - 1],
                        ag_r.at[j, stage, col, d - 1],
                        partner(axis, d),
                    )
                )
        return copies

    scatters = [[scatter(j, stage) for stage in range(3)] for j in range(2)]
    spreads = [[spread(j, stage) for stage in range(3)] for j in range(2)]

    def arrived(copies):
        for copy in copies:
            copy.wait_recv()

    def begin(copies):
        for copy in copies:
            copy.start()

    def next_scatter(j, stage):
        arrived(scatters[j][stage])
        for col in range(2):
            if stage < 2:
                sources[stage + 1][j, col] = gathered(j, stage, col)
            else:
                red[col, j, first_owner(2, col)] = (gathered(j, 2, col) * scale).astype(BF16)
        begin(scatters[j][stage + 1] if stage < 2 else spreads[j][2])

    def next_spread(j, stage):
        arrived(spreads[j][stage])
        begin(spreads[j][stage - 1])

    scale = 1.0 / math.sqrt(blocks * BLK)
    lax.fori_loop(0, 4, head, 0)

    mix[c] = (nn(o_s[0], wo[0]) + nn(o_s[1], wo[1])).astype(BF16)
    to_sib = [
        remote(ref.at[c], ref.at[c], ms.at[n], mr.at[n], sib) for n, ref in enumerate((mix, gtb))
    ]
    to_sib[0].start()
    for part in range(3):
        cols = slice(part * BLK, (part + 1) * BLK)
        total = jnp.zeros((D, BLK), F32)
        for slot in range(2):
            total = total + nn(wk[slot], dkT_s[slot, :, :, cols].reshape(BLK, BLK))
            total = total + nn(wv[slot], dvT_s[slot, :, :, cols].reshape(BLK, BLK))
        if part == 0:
            ct_send[0] = total.astype(BF16)
        else:
            ct_own[part - 1] = total
    terms = [
        remote(ct_send.at[n], ct_recv.at[n], cs.at[n], cr.at[n], prev1) for n in range(2)
    ]

    next_scatter(0, 0)
    next_scatter(0, 1)
    next_scatter(1, 0)
    terms[0].start()
    gtq = nt(dq_s[0], wq[0]) + nt(dq_s[1], wq[1])
    next_scatter(0, 2)
    next_scatter(1, 1)
    terms[0].wait_recv()
    ct_send[1] = (ct_own[0] + ct_recv[0].astype(F32)).astype(BF16)
    terms[1].start()
    next_spread(0, 2)
    next_scatter(1, 2)
    terms[1].wait_recv()
    gtb[c] = (gtq + jnp.transpose(ct_own[1] + ct_recv[1].astype(F32))).astype(BF16)
    to_sib[1].start()
    next_spread(0, 1)
    next_spread(1, 2)
    next_spread(1, 1)
    arrived(to_sib)
    arrived(spreads[0][0])
    arrived(spreads[1][0])
    sent = mine + onward + times + [decays] + weights + psends + terms + to_sib
    for j in range(2):
        for stage in range(3):
            sent += scatters[j][stage] + spreads[j][stage]
    for copy in sent:
        copy.wait_send()


def finish(mix, gtb, red, mixed, gt, grad_q, grad_k, grad_v, grad_o, wide, rows, sem):
    copies = [
        pltpu.make_async_copy(mix, mixed, sem.at[0]),
        pltpu.make_async_copy(gtb, gt, sem.at[1]),
    ]
    copies[0].start()
    copies[1].start()
    for n, out in enumerate((grad_q, grad_k, grad_v, grad_o)):
        half = pl.ds((n % 2) * (D // 8), D // 8)
        for j in range(2):
            val = red[n // 2, j, half].astype(F32).reshape(D, HD)
            if n < 3:
                wide[n, :, j * HD : (j + 1) * HD] = val
            else:
                for k in range(4):
                    rows[j * HD : (j + 1) * HD, k * HD : (k + 1) * HD] = val[k * HD : (k + 1) * HD]
        copies.append(pltpu.make_async_copy(wide.at[n] if n < 3 else rows, out, sem.at[2 + n]))
        copies[-1].start()
    for copy in copies:
        copy.wait()


def shards(table, cotangent, stamps, starts, w_query, w_key, w_value, w_out, decay):
    tm_size = lax.axis_size("tm")
    hbm = pl.BlockSpec(memory_space=pltpu.HBM)
    vmem = pl.BlockSpec(memory_space=pltpu.VMEM)
    dma = pltpu.SemaphoreType.DMA
    V = pltpu.VMEM
    near = (
        V((2, BLK, D), BF16),
        V((2, BLK, D), BF16),
        V((2, 2, 128, 8, 128), BF16),
    )
    near = pl.pallas_call(
        functools.partial(kernel, tm_size),
        out_shape=near,
        in_specs=[hbm] * 9,
        out_specs=(vmem, vmem, vmem),
        scratch_shapes=[
            V((3, BLK, D), BF16),
            V((D, WIN), BF16),
            V((BLK, D), BF16),
            V((2, BLK), jnp.int32),
            V((2, BLK), jnp.int32),
            pltpu.SMEM((1, 2), F32),
            V((2, 2, BLK), jnp.int32),
            V((8, 128), F32),
            V((8, 128), F32),
            V((2, D, BLK), BF16),
            V((2, D, BLK), BF16),
            V((2, D, BLK), BF16),
            V((2, BLK, D), BF16),
            V((BLK, WIN), F32),
            V((4, 1, WIN), F32),
            V((4, BLK, HD), BF16),
            V((4, HD, BLK), BF16),
            V((4, WIN, HD), BF16),
            V((4, WIN, HD), BF16),
            V((4, BLK, HD), BF16),
            V((4, HD, BLK), BF16),
            V((2, BLK, BLK), BF16),
            V((2, BLK, BLK), BF16),
            V((2, 2, HD, WIN), BF16),
            V((2, 2, HD, WIN), BF16),
            V((2, 4, D, 128), F32),
            V((2, 4, D, 128), F32),
            V((4, D, 128), F32),
            V((2, 2, 2 * D, 128), BF16),
            V((2, 2, D // 2, 128), F32),
            V((2, 2, D // 8, 128), F32),
            V((2, 2, 3, D // 2, 128), BF16),
            V((2, 2, 3, D // 8, 128), F32),
            V((2, 2, 7, 8, 128), F32),
            V((2, D, BLK), BF16),
            V((2, D, BLK), BF16),
            V((2, D, BLK), F32),
            dma((9,)),
            dma((6,)),
            dma((6,)),
            dma((5,)),
            dma((5,)),
            dma((2,)),
            dma((2,)),
            dma((2, 3, 2, 7)),
            dma((2, 3, 2, 7)),
            dma((2, 3, 2, 7)),
            dma((2, 3, 2, 7)),
            dma((2,)),
            dma((2,)),
            dma((2,)),
            dma((2,)),
        ],
        compiler_params=pltpu.CompilerParams(
            collective_id=0, has_side_effects=True, vmem_limit_bytes=58 * 1024 * 1024
        ),
        name="history_attention",
    )(table, cotangent, stamps, starts, w_query, w_key, w_value, w_out, decay.reshape(1, 2))
    shapes = ((2, BLK, D), (2, BLK, D), (D, BLK), (D, BLK), (D, BLK), (BLK, D))
    return pl.pallas_call(
        finish,
        out_shape=tuple(
            jax.ShapeDtypeStruct(shape, BF16 if n < 2 else F32) for n, shape in enumerate(shapes)
        ),
        in_specs=[vmem] * 3,
        out_specs=(hbm,) * 6,
        scratch_shapes=[V((3, D, BLK), F32), V((BLK, D), F32), dma((6,))],
        compiler_params=pltpu.CompilerParams(vmem_limit_bytes=16 * 1024 * 1024),
        name="finish",
    )(*near)


def solution(mesh):
    return jax.shard_map(
        shards,
        mesh=mesh,
        in_specs=(
            P(None, "tm", None),
            P(None, "tm", None),
            P(None, "tm"),
            P(None, "tm"),
            P(None, "rep"),
            P(None, "rep"),
            P(None, "rep"),
            P("rep", None),
            P("rep"),
        ),
        out_specs=(
            P(None, "tm", None),
            P(None, "tm", None),
            P(None, "rep"),
            P(None, "rep"),
            P(None, "rep"),
            P("rep", None),
        ),
        check_vma=False,
    )
```

time: 79 us -> 67.7 us (0.86)
  local copies, waits for them, and re-layouts: 5.83 us -> 0 us
  Pallas kernels: 72.2 us -> 67 us
    pallas_call x1 -> x2, Pallas kernels: 72.2 us -> 67 us  [the longest x1 65.3 us: shards(): pl.pallas_call(functools.partial(kernel, tm_size), out_shape=near, in_spe...]
    unnamed x10 -> x0, local copies, waits for them, and re-layouts: 2.53 us -> none
    reshape x2 -> x0, local copies, waits for them, and re-layouts: 1.88 us -> none  [wide(): return jnp.transpose(part, (1, 0, 2)).reshape(D, 256)]
    slice x1 -> x0, local copies, waits for them, and re-layouts: 1.07 us -> none  [shards(): red[3].reshape(2, 4, 128, 128)]
where the time goes in v2:
time: 67.7 us; the launch traced here: 67.6 us
  Pallas kernels  67 us (99%)
    pallas_call x1, Pallas kernels, shards(): pl.pallas_call(functools.partial(kernel, tm_size), out_shape=near, in_spe...  65.3 us
    pallas_call x1, Pallas kernels, shards(): pl.pallas_call(finish, out_shape=tuple((jax.ShapeDtypeStruct(shape, BF16...  1.71 us

profile of v2, /device:TPU:32, one launch (start us, length us, event | category | flops | bytes accessed | tf_op | source)
XLA Modules:
  0.0 67.6 jit_solution(3365202221760203608)
XLA Ops:
  0.6 65.3 %history_attention.1 = (bf16[2,256,512]{2,1,0:T(8,128)(2,1)S(1)}, bf16[2,256,512]{2,1,0:T(8,128)(2,1)S(1)}, bf16[2,2,128,8,128]{4,3,2,1,0:T(8,128)(2,1)S(1)}) custom-call(bf16[2,256,512]{2,1,0:T(8,128)(2,1)} %table.1, bf16[2,256,512]{2,1,0:T(8,128)(2,1)} %cot.1, s32[2,256]{1,0:T(2,128)} %stamps.1, s32[2,256]{1,0:T(2,128)} %starts.1, bf16[512,256]{1,0:T(8,128)(2,1)} %wq_in.1, ...), custom_call_target="tpu_custom_call" | custom-call | tf_op jit(solution)/shard_map/history_attention/pallas_call | solution.py:464
  65.9 1.7 %finish.1 = (bf16[2,256,512]{2,1,0:T(8,128)(2,1)}, bf16[2,256,512]{2,1,0:T(8,128)(2,1)}, f32[512,256]{1,0:T(8,128)}, f32[512,256]{1,0:T(8,128)}, f32[512,256]{1,0:T(8,128)}, /*index=5*/f32[256,512]{1,0:T(8,128)}) custom-call(bf16[2,256,512]{2,1,0:T(8,128)(2,1)S(1)} %get-tuple-element.9.mix, bf16[2,256,512]{2,1,0:T(8,128)(2,1)S(1)} %get-tuple-element.10.gtb, ...), custom_call_target="tpu_custom_call" | custom-call | tf_op jit(solution)/shard_map/finish/pallas_call | solution.py:529

commit v3 on v2

--- a/solution.py
+++ b/solution.py
@@ -13,12 +13,14 @@
 WIN = 3 * BLK
 D = 512
 NX, NY, NZ = 4, 4, 8
+CHUNKS = 4
 LOG2E = 1.4426950408889634
 MESH = pl.DeviceIdType.MESH
 F32 = jnp.float32
 BF16 = jnp.bfloat16
 ORDERS = (("x", "y", "z"), ("y", "x", "z"))
 SIZES = {"x": NX, "y": NY, "z": NZ}
+FARTHEST = {4: (2, 1, 3), 8: (4, 3, 5, 2, 6, 1, 7)}
 
 
 def nt(a, b):
@@ -66,8 +68,7 @@
     doT_s,
     o_s,
     dq_s,
-    dkT_s,
-    dvT_s,
+    kvT_s,
     psend,
     precv,
     pown,
@@ -95,6 +96,7 @@
     cr,
     ms,
     mr,
+    met,
 ):
     tm = lax.axis_index("tm")
     c = lax.axis_index("rep")
@@ -108,21 +110,19 @@
 
     def partner(axis, d):
         at = dict(coord)
-        at[axis] = (coord[axis] + d) % SIZES[axis]
+        at[axis] = (coord[axis] + SIZES[axis] + d) % SIZES[axis]
         return ((at["x"] * NZ + at["z"]) * NY + at["y"], c)
 
     next1 = holder((blk + 1) % blocks)
-    next2 = holder((blk + 2) % blocks)
     pos1 = (blk + blocks - 1) % blocks
     pos2 = (blk + blocks - 2) % blocks
     prev1 = holder(pos1)
-    prev2 = holder(pos2)
     sib = (tm, 1 - c)
 
     barrier = pltpu.get_barrier_semaphore()
-    friends = [next1, next2, prev1, prev2, sib]
-    for axis, size in SIZES.items():
-        friends += [partner(axis, d) for d in range(1, size)]
+    friends = [next1, prev1, sib]
+    for axis in SIZES:
+        friends += [partner(axis, 1), partner(axis, -1)]
     for friend in friends:
         pl.semaphore_signal(barrier, inc=1, device_id=friend, device_id_type=MESH)
 
@@ -150,10 +150,45 @@
             src_ref=src, dst_ref=dst, send_sem=send, recv_sem=recv, device_id=to, device_id_type=MESH
         )
 
+    pl.semaphore_wait(barrier, len(friends))
+
+    def tell(token):
+        axis, d, n = token
+        pl.semaphore_signal(met.at[n], inc=1, device_id=partner(axis, d), device_id_type=MESH)
+
+    def hear(token):
+        pl.semaphore_wait(met.at[token[2]], 1)
+
+    tokens = ([("x", 1, 0), ("y", 1, 1), ("z", 1, 2), ("z", -1, 3)], [("z", 1, 4), ("z", -1, 5)], [("z", 1, 6)])
+
+    chunk = BLK // CHUNKS
+    pieces = [pl.ds(n * chunk, chunk) for n in range(CHUNKS)]
+    mine = [
+        remote(table.at[c, rows], xw.at[1, rows], hs.at[n], hr.at[n], next1)
+        for n, rows in enumerate(pieces)
+    ]
+    onward = [
+        remote(xw.at[1, rows], xw.at[0, rows], hs.at[CHUNKS + n], hr.at[CHUNKS + n], next1)
+        for n, rows in enumerate(pieces)
+    ]
+    times = [
+        remote(src, ts_near.at[n], hs.at[2 * CHUNKS + n], hr.at[2 * CHUNKS + n], next1)
+        for n, src in enumerate((stamps, ts_near.at[0]))
+    ]
+    weights = [
+        remote(src, dst.at[0], ws.at[n], wr.at[n], sib)
+        for n, (src, dst) in enumerate(((wq_in, wq), (wk_in, wk), (wv_in, wv), (wo_in, wo)))
+    ]
+    decays = remote(dec_send, dec_recv, ws.at[4], wr.at[4], sib)
+    for copy in times[:1] + mine + weights:
+        copy.start()
+    for token in tokens[0]:
+        tell(token)
     for copy in loads[:3]:
         copy.wait()
     sub = lax.broadcasted_iota(jnp.int32, (8, 128), 0)
     dec_send[...] = jnp.where(sub == 0, dec_in[0, 0], dec_in[0, 1])
+    decays.start()
     first_row = jnp.where(c == 0, st_own[0:1, :], st_own[1:2, :]) - (blk - 2) * BLK
     first_col = jnp.transpose(jnp.broadcast_to(first_row.astype(F32), (128, BLK)))
     row_id = lax.broadcasted_iota(jnp.int32, (BLK, 128), 0)
@@ -163,34 +198,11 @@
         ok = (key_id.astype(F32) >= first_col) & (key_id <= row_id + 2 * BLK)
         mb[:, n * 128 : (n + 1) * 128] = jnp.where(ok, 0.0, -1e30)
 
-    pl.semaphore_wait(barrier, len(friends))
-
-    half = BLK // 2
-    top, low = pl.ds(0, half), pl.ds(half, half)
-    mine = [
-        remote(table.at[c, rows], xw.at[1, rows], hs.at[n], hr.at[n], next1)
-        for n, rows in enumerate((top, low))
-    ]
-    onward = [
-        remote(xw.at[1, rows], xw.at[0, rows], hs.at[2 + n], hr.at[2 + n], next1)
-        for n, rows in enumerate((top, low))
-    ]
-    times = [
-        remote(stamps, ts_near.at[n], hs.at[4 + n], hr.at[4 + n], to)
-        for n, to in enumerate((next1, next2))
-    ]
-    weights = [
-        remote(src, dst.at[0], ws.at[n], wr.at[n], sib)
-        for n, (src, dst) in enumerate(((wq_in, wq), (wk_in, wk), (wv_in, wv), (wo_in, wo)))
-    ]
-    decays = remote(dec_send, dec_recv, ws.at[4], wr.at[4], sib)
-    for copy in mine + times + [decays] + weights:
-        copy.start()
 
     def put_heads(dst, slot, rows, val):
         val = val.astype(BF16)
         for j in range(2):
-            dst[2 * j + slot, rows, :] = val[:, j * HD : (j + 1) * HD]
+            dst[2 * slot + j, rows, :] = val[:, j * HD : (j + 1) * HD]
         return val
 
     every = pl.ds(0, BLK)
@@ -199,10 +211,10 @@
         x = xw[2]
         val = put_heads(q_s, slot, every, nn(x, wq[slot]))
         for j in range(2):
-            qT_s[2 * j + slot] = jnp.transpose(val[:, j * HD : (j + 1) * HD])
+            qT_s[2 * slot + j] = jnp.transpose(val[:, j * HD : (j + 1) * HD])
         val = put_heads(do_s, slot, every, nt(g_s[...], wo[slot]))
         for j in range(2):
-            doT_s[2 * j + slot] = jnp.transpose(val[:, j * HD : (j + 1) * HD])
+            doT_s[2 * slot + j] = jnp.transpose(val[:, j * HD : (j + 1) * HD])
 
     def keys_of(part, slot):
         rows = pl.ds(part * BLK, BLK)
@@ -214,9 +226,19 @@
     own_rows(1)
     keys_of(2, 1)
     xT[:, 2 * BLK :] = jnp.transpose(xw[2])
-    for n in range(2):
+    times[0].wait_recv()
+    times[1].start()
+    for token in tokens[0]:
+        hear(token)
+    for token in tokens[1]:
+        tell(token)
+    for n in range(CHUNKS):
         mine[n].wait_recv()
         onward[n].start()
+    for token in tokens[1]:
+        hear(token)
+    for token in tokens[2]:
+        tell(token)
     keys_of(1, 1)
     xT[:, BLK : 2 * BLK] = jnp.transpose(xw[1])
     for copy in weights:
@@ -224,7 +246,9 @@
     own_rows(0)
     keys_of(2, 0)
     keys_of(1, 0)
-    for copy in times + [decays]:
+    for token in tokens[2]:
+        hear(token)
+    for copy in (times[1], decays):
         copy.wait_recv()
     for copy in onward:
         copy.wait_recv()
@@ -242,60 +266,59 @@
     )
     rel = (rel - base).astype(F32) * LOG2E
     for j in range(2):
-        brow[2 * j] = rel * dec_recv[j : j + 1, 0:1]
-        brow[2 * j + 1] = rel * dec_send[j : j + 1, 0:1]
+        brow[j] = rel * dec_recv[j : j + 1, 0:1]
+        brow[2 + j] = rel * dec_send[j : j + 1, 0:1]
 
     inv_scale = 1.0 / math.sqrt(HD)
     psends = [
         remote(psend.at[j], precv.at[j], ps.at[j], pr.at[j], sib) for j in range(2)
     ]
 
-    def head(t, carry):
-        slot = t % 2
-        j = t // 2
-        lanes = pl.ds(pl.multiple_of(j * HD, HD), HD)
-        s = nt(q_s[t], k_s[t]) * (inv_scale * LOG2E) + (mb[...] + brow[t])
+    def products(t):
+        return nt(q_s[t], k_s[t]), nt(do_s[t], v_s[t])
+
+    def softmax(t, s, dp):
+        s = s * (inv_scale * LOG2E) + (mb[...] + brow[t])
         p = jnp.exp2(s - jnp.max(s, axis=-1, keepdims=True))
         p = p * (1.0 / jnp.sum(p, axis=-1, keepdims=True))
-        pb = p.astype(BF16)
-        o = nn(pb, v_s[t]).astype(BF16)
-        o_s[slot, :, lanes] = o
-        dvT = nn(doT_s[t], pb).astype(BF16)
-        dvT_s[slot, j] = dvT
-        dp = nt(do_s[t], v_s[t])
         delta = jnp.sum(p * dp, axis=-1, keepdims=True)
-        ds = (p * (dp - delta)).astype(BF16)
-        dq = (nn(ds, k_s[t]) * inv_scale).astype(BF16)
-        dq_s[slot, :, lanes] = dq
-        dkT = (nn(qT_s[t], ds) * inv_scale).astype(BF16)
-        dkT_s[slot, j] = dkT
-        parts = [
-            nn(xT[:, 2 * BLK :], dq),
-            nt(xT[...], dkT),
-            nt(xT[...], dvT),
-        ]
-        go = nn(jnp.transpose(o), g_s[...])
-        for n in range(3):
-            pown[n] = parts[n]
+        return p.astype(BF16), (p * (dp - delta)).astype(BF16)
+
+    def attention(t, pb, ds):
+        lanes = slice((t % 2) * HD, (t % 2 + 1) * HD)
+        o_s[t // 2, :, lanes] = nn(pb, v_s[t]).astype(BF16)
+        dq_s[t // 2, :, lanes] = (nn(ds, k_s[t]) * inv_scale).astype(BF16)
+        kvT_s[t, :HD, :] = (nn(qT_s[t], ds) * inv_scale).astype(BF16)
+        kvT_s[t, HD:, :] = nn(doT_s[t], pb).astype(BF16)
+
+    def weight_grads(t):
+        lanes = slice((t % 2) * HD, (t % 2 + 1) * HD)
+        kv = nt(xT[...], kvT_s[t])
+        go = nn(jnp.transpose(o_s[t // 2, :, lanes]), g_s[...])
+        to = psend.at[t] if t < 2 else pown.at[t - 2]
+        to[0] = nn(xT[:, 2 * BLK :], dq_s[t // 2, :, lanes]).astype(to.dtype)
+        to[1] = kv[:, :HD].astype(to.dtype)
+        to[2] = kv[:, HD:].astype(to.dtype)
         for n in range(4):
-            pown[3, n * HD : (n + 1) * HD, :] = go[:, n * HD : (n + 1) * HD]
-
-        for jj in range(2):
-
-            @pl.when(t == 2 * jj)
-            def _():
-                psend[jj] = pown[...]
-                psends[jj].start()
-
-            @pl.when(t == 2 * jj + 1)
-            def _():
-                psends[jj].wait_recv()
-                for n in range(4):
-                    b0[jj, n // 2, (n % 2) * D : (n % 2 + 1) * D, :] = (pown[n] + precv[jj, n]).astype(BF16)
-                for copy in scatters[jj][0]:
-                    copy.start()
-
-        return carry
+            to[3, n * HD : (n + 1) * HD, :] = go[:, n * HD : (n + 1) * HD].astype(to.dtype)
+
+    def reduce_pair(j):
+        psends[j].wait_recv()
+        for n in range(4):
+            b0[j, n // 2, (n % 2) * D : (n % 2 + 1) * D, :] = (pown[j, n] + precv[j, n].astype(F32)).astype(BF16)
+        begin(scatters[j][0])
+
+    def pass_on(step):
+        if step in (0, 2):
+            psends[step // 2].start()
+        if step == 3:
+            reduce_pair(1)
+        if step in (1, 2):
+            pl.when(c == step - 1)(lambda: reduce_pair(0))
+
+    def begin(copies):
+        for copy in copies:
+            copy.start()
 
     sources = (b0, b1, b2)
     landing = (rc0, rc1, rc2)
@@ -309,7 +332,7 @@
         copies = []
         for col in range(2):
             axis, size, piece = place(stage, col)
-            for d in range(1, size):
+            for d in FARTHEST[size]:
                 there = (coord[axis] + d) % size
                 copies.append(
                     remote(
@@ -341,7 +364,7 @@
         for col in range(2):
             axis, size, piece = place(stage, col)
             here = pl.ds(first_owner(stage, col), piece // 8)
-            for d in range(1, size):
+            for d in FARTHEST[size]:
                 copies.append(
                     remote(
                         red.at[col, j, here],
@@ -360,15 +383,11 @@
         for copy in copies:
             copy.wait_recv()
 
-    def begin(copies):
-        for copy in copies:
-            copy.start()
-
     def next_scatter(j, stage):
         arrived(scatters[j][stage])
         for col in range(2):
             if stage < 2:
-                sources[stage + 1][j, col] = gathered(j, stage, col)
+                sources[stage + 1][j, col] = gathered(j, stage, col).astype(sources[stage + 1].dtype)
             else:
                 red[col, j, first_owner(2, col)] = (gathered(j, 2, col) * scale).astype(BF16)
         begin(scatters[j][stage + 1] if stage < 2 else spreads[j][2])
@@ -378,7 +397,19 @@
         begin(spreads[j][stage - 1])
 
     scale = 1.0 / math.sqrt(blocks * BLK)
-    lax.fori_loop(0, 4, head, 0)
+    turn = (0, 2, 1, 3)
+    now = products(turn[0])
+    for step in range(4):
+        later = products(turn[step + 1]) if step < 3 else None
+        if step > 0:
+            weight_grads(turn[step - 1])
+        pb, ds = softmax(turn[step], *now)
+        if step > 0:
+            pass_on(step - 1)
+        attention(turn[step], pb, ds)
+        now = later
+    weight_grads(turn[3])
+    pass_on(3)
 
     mix[c] = (nn(o_s[0], wo[0]) + nn(o_s[1], wo[1])).astype(BF16)
     to_sib = [
@@ -388,39 +419,46 @@
     for part in range(3):
         cols = slice(part * BLK, (part + 1) * BLK)
         total = jnp.zeros((D, BLK), F32)
-        for slot in range(2):
-            total = total + nn(wk[slot], dkT_s[slot, :, :, cols].reshape(BLK, BLK))
-            total = total + nn(wv[slot], dvT_s[slot, :, :, cols].reshape(BLK, BLK))
+        for t in range(4):
+            lanes = slice((t % 2) * HD, (t % 2 + 1) * HD)
+            both = jnp.concatenate([wk[t // 2, :, lanes], wv[t // 2, :, lanes]], axis=1)
+            total = total + nn(both, kvT_s[t, :, cols])
         if part == 0:
             ct_send[0] = total.astype(BF16)
         else:
             ct_own[part - 1] = total
     terms = [
-        remote(ct_send.at[n], ct_recv.at[n], cs.at[n], cr.at[n], prev1) for n in range(2)
+        [
+            remote(ct_send.at[n, rows], ct_recv.at[n, rows], cs.at[n, h], cr.at[n, h], prev1)
+            for h, rows in enumerate((every, pl.ds(BLK, BLK)))
+        ]
+        for n in range(2)
     ]
 
     next_scatter(0, 0)
+    next_scatter(1, 0)
+    gtq = nt(dq_s[0], wq[0]) + nt(dq_s[1], wq[1])
     next_scatter(0, 1)
-    next_scatter(1, 0)
-    terms[0].start()
-    gtq = nt(dq_s[0], wq[0]) + nt(dq_s[1], wq[1])
+    next_scatter(1, 1)
+    begin(terms[0])
     next_scatter(0, 2)
-    next_scatter(1, 1)
-    terms[0].wait_recv()
-    ct_send[1] = (ct_own[0] + ct_recv[0].astype(F32)).astype(BF16)
-    terms[1].start()
+    next_scatter(1, 2)
+    for h in range(2):
+        terms[0][h].wait_recv()
+        rows = slice(h * BLK, (h + 1) * BLK)
+        ct_send[1, rows, :] = (ct_own[0, rows, :] + ct_recv[0, rows, :].astype(F32)).astype(BF16)
+        terms[1][h].start()
     next_spread(0, 2)
-    next_scatter(1, 2)
-    terms[1].wait_recv()
+    next_spread(1, 2)
+    next_spread(0, 1)
+    arrived(terms[1])
     gtb[c] = (gtq + jnp.transpose(ct_own[1] + ct_recv[1].astype(F32))).astype(BF16)
     to_sib[1].start()
-    next_spread(0, 1)
-    next_spread(1, 2)
     next_spread(1, 1)
     arrived(to_sib)
     arrived(spreads[0][0])
     arrived(spreads[1][0])
-    sent = mine + onward + times + [decays] + weights + psends + terms + to_sib
+    sent = mine + onward + times + [decays] + weights + psends + terms[0] + terms[1] + to_sib
     for j in range(2):
         for stage in range(3):
             sent += scatters[j][stage] + spreads[j][stage]
@@ -490,23 +528,22 @@
             V((4, HD, BLK), BF16),
             V((2, BLK, BLK), BF16),
             V((2, BLK, BLK), BF16),
-            V((2, 2, HD, WIN), BF16),
-            V((2, 2, HD, WIN), BF16),
+            V((4, 2 * HD, WIN), BF16),
+            V((2, 4, D, 128), BF16),
+            V((2, 4, D, 128), BF16),
             V((2, 4, D, 128), F32),
-            V((2, 4, D, 128), F32),
-            V((4, D, 128), F32),
             V((2, 2, 2 * D, 128), BF16),
-            V((2, 2, D // 2, 128), F32),
+            V((2, 2, D // 2, 128), BF16),
             V((2, 2, D // 8, 128), F32),
             V((2, 2, 3, D // 2, 128), BF16),
-            V((2, 2, 3, D // 8, 128), F32),
+            V((2, 2, 3, D // 8, 128), BF16),
             V((2, 2, 7, 8, 128), F32),
             V((2, D, BLK), BF16),
             V((2, D, BLK), BF16),
             V((2, D, BLK), F32),
             dma((9,)),
-            dma((6,)),
-            dma((6,)),
+            dma((2 * CHUNKS + 2,)),
+            dma((2 * CHUNKS + 2,)),
             dma((5,)),
             dma((5,)),
             dma((2,)),
@@ -515,10 +552,11 @@
             dma((2, 3, 2, 7)),
             dma((2, 3, 2, 7)),
             dma((2, 3, 2, 7)),
+            dma((2, 2)),
+            dma((2, 2)),
             dma((2,)),
             dma((2,)),
-            dma((2,)),
-            dma((2,)),
+            pltpu.SemaphoreType.REGULAR((7,)),
         ],
         compiler_params=pltpu.CompilerParams(
             collective_id=0, has_side_effects=True, vmem_limit_bytes=58 * 1024 * 1024

time: 67.7 us -> 62.2 us (0.919)
  the two profiles are of different devices: /device:TPU:32 before, /device:TPU:1 now
where the time goes in v3:
time: 62.2 us; the launch traced here: 62.1 us
  Pallas kernels  61.5 us (99%)
  between operations  0.64 us (1%)
    pallas_call x1, Pallas kernels, shards(): pl.pallas_call(functools.partial(kernel, tm_size), out_shape=near, in_spe...  59.8 us
    pallas_call x1, Pallas kernels, shards(): pl.pallas_call(finish, out_shape=tuple((jax.ShapeDtypeStruct(shape, BF16...  1.71 us

profile of v3, /device:TPU:1, one launch (start us, length us, event | category | flops | bytes accessed | tf_op | source)
XLA Modules:
  0.0 62.1 jit_solution(9712489447527827640)
XLA Ops:
  0.6 59.8 %history_attention.1 = (bf16[2,256,512]{2,1,0:T(8,128)(2,1)S(1)}, bf16[2,256,512]{2,1,0:T(8,128)(2,1)S(1)}, bf16[2,2,128,8,128]{4,3,2,1,0:T(8,128)(2,1)S(1)}) custom-call(bf16[2,256,512]{2,1,0:T(8,128)(2,1)} %table.1, bf16[2,256,512]{2,1,0:T(8,128)(2,1)} %cot.1, s32[2,256]{1,0:T(2,128)} %stamps.1, s32[2,256]{1,0:T(2,128)} %starts.1, bf16[512,256]{1,0:T(8,128)(2,1)} %wq_in.1, ...), custom_call_target="tpu_custom_call" | custom-call | tf_op jit(solution)/shard_map/history_attention/pallas_call | solution.py:502
  60.4 1.7 %finish.1 = (bf16[2,256,512]{2,1,0:T(8,128)(2,1)}, bf16[2,256,512]{2,1,0:T(8,128)(2,1)}, f32[512,256]{1,0:T(8,128)}, f32[512,256]{1,0:T(8,128)}, f32[512,256]{1,0:T(8,128)}, /*index=5*/f32[256,512]{1,0:T(8,128)}) custom-call(bf16[2,256,512]{2,1,0:T(8,128)(2,1)S(1)} %get-tuple-element.9.mix, bf16[2,256,512]{2,1,0:T(8,128)(2,1)S(1)} %get-tuple-element.10.gtb, ...), custom_call_target="tpu_custom_call" | custom-call | tf_op jit(solution)/shard_map/finish/pallas_call | solution.py:567

commit v4 on v3

--- a/solution.py
+++ b/solution.py
@@ -150,6 +150,8 @@
             src_ref=src, dst_ref=dst, send_sem=send, recv_sem=recv, device_id=to, device_id_type=MESH
         )
 
+    for copy in loads[:4]:
+        copy.wait()
     pl.semaphore_wait(barrier, len(friends))
 
     def tell(token):
@@ -164,7 +166,7 @@
     chunk = BLK // CHUNKS
     pieces = [pl.ds(n * chunk, chunk) for n in range(CHUNKS)]
     mine = [
-        remote(table.at[c, rows], xw.at[1, rows], hs.at[n], hr.at[n], next1)
+        remote(xw.at[2, rows], xw.at[1, rows], hs.at[n], hr.at[n], next1)
         for n, rows in enumerate(pieces)
     ]
     onward = [
@@ -176,16 +178,14 @@
         for n, src in enumerate((stamps, ts_near.at[0]))
     ]
     weights = [
-        remote(src, dst.at[0], ws.at[n], wr.at[n], sib)
-        for n, (src, dst) in enumerate(((wq_in, wq), (wk_in, wk), (wv_in, wv), (wo_in, wo)))
+        remote(src.at[1], dst.at[0], ws.at[n], wr.at[n], sib)
+        for n, (src, dst) in enumerate(((wq, wq), (wk, wk), (wv, wv), (wo, wo)))
     ]
     decays = remote(dec_send, dec_recv, ws.at[4], wr.at[4], sib)
-    for copy in times[:1] + mine + weights:
+    for copy in times[:1] + mine:
         copy.start()
     for token in tokens[0]:
         tell(token)
-    for copy in loads[:3]:
-        copy.wait()
     sub = lax.broadcasted_iota(jnp.int32, (8, 128), 0)
     dec_send[...] = jnp.where(sub == 0, dec_in[0, 0], dec_in[0, 1])
     decays.start()
@@ -199,6 +199,10 @@
         mb[:, n * 128 : (n + 1) * 128] = jnp.where(ok, 0.0, -1e30)
 
 
+    def begin(copies):
+        for copy in copies:
+            copy.start()
+
     def put_heads(dst, slot, rows, val):
         val = val.astype(BF16)
         for j in range(2):
@@ -221,8 +225,9 @@
         put_heads(k_s, slot, rows, nn(xw[part], wk[slot]))
         put_heads(v_s, slot, rows, nn(xw[part], wv[slot]))
 
-    for copy in loads[3:]:
+    for copy in loads[4:]:
         copy.wait()
+    begin(weights)
     own_rows(1)
     keys_of(2, 1)
     xT[:, 2 * BLK :] = jnp.transpose(xw[2])
@@ -316,10 +321,6 @@
         if step in (1, 2):
             pl.when(c == step - 1)(lambda: reduce_pair(0))
 
-    def begin(copies):
-        for copy in copies:
-            copy.start()
-
     sources = (b0, b1, b2)
     landing = (rc0, rc1, rc2)
     rows_at = (2 * D, D // 2, D // 8)
@@ -439,15 +440,15 @@
     next_scatter(1, 0)
     gtq = nt(dq_s[0], wq[0]) + nt(dq_s[1], wq[1])
     next_scatter(0, 1)
+    begin(terms[0])
     next_scatter(1, 1)
-    begin(terms[0])
     next_scatter(0, 2)
-    next_scatter(1, 2)
     for h in range(2):
         terms[0][h].wait_recv()
         rows = slice(h * BLK, (h + 1) * BLK)
         ct_send[1, rows, :] = (ct_own[0, rows, :] + ct_recv[0, rows, :].astype(F32)).astype(BF16)
         terms[1][h].start()
+    next_scatter(1, 2)
     next_spread(0, 2)
     next_spread(1, 2)
     next_spread(0, 1)

time: 62.2 us -> 60.1 us (0.966)
  the two profiles are of different devices: /device:TPU:1 before, /device:TPU:32 now
where the time goes in v4:
time: 60.1 us; the launch traced here: 59.7 us
  Pallas kernels  59 us (98%)
  between operations  0.64 us (1%)
    pallas_call x1, Pallas kernels, shards(): pl.pallas_call(functools.partial(kernel, tm_size), out_shape=near, in_spe...  57.3 us
    pallas_call x1, Pallas kernels, shards(): pl.pallas_call(finish, out_shape=tuple((jax.ShapeDtypeStruct(shape, BF16...  1.71 us

profile of v4, /device:TPU:32, one launch (start us, length us, event | category | flops | bytes accessed | tf_op | source)
XLA Modules:
  0.0 59.7 jit_solution(17512290408525419270)
XLA Ops:
  0.6 57.3 %history_attention.1 = (bf16[2,256,512]{2,1,0:T(8,128)(2,1)S(1)}, bf16[2,256,512]{2,1,0:T(8,128)(2,1)S(1)}, bf16[2,2,128,8,128]{4,3,2,1,0:T(8,128)(2,1)S(1)}) custom-call(bf16[2,256,512]{2,1,0:T(8,128)(2,1)} %table.1, bf16[2,256,512]{2,1,0:T(8,128)(2,1)} %cot.1, s32[2,256]{1,0:T(2,128)} %stamps.1, s32[2,256]{1,0:T(2,128)} %starts.1, bf16[512,256]{1,0:T(8,128)(2,1)} %wq_in.1, ...), custom_call_target="tpu_custom_call" | custom-call | tf_op jit(solution)/shard_map/history_attention/pallas_call | solution.py:503
  58.0 1.7 %finish.1 = (bf16[2,256,512]{2,1,0:T(8,128)(2,1)}, bf16[2,256,512]{2,1,0:T(8,128)(2,1)}, f32[512,256]{1,0:T(8,128)}, f32[512,256]{1,0:T(8,128)}, f32[512,256]{1,0:T(8,128)}, /*index=5*/f32[256,512]{1,0:T(8,128)}) custom-call(bf16[2,256,512]{2,1,0:T(8,128)(2,1)S(1)} %get-tuple-element.9.mix, bf16[2,256,512]{2,1,0:T(8,128)(2,1)S(1)} %get-tuple-element.10.gtb, ...), custom_call_target="tpu_custom_call" | custom-call | tf_op jit(solution)/shard_map/finish/pallas_call | solution.py:568

commit v5 on v4

--- a/solution.py
+++ b/solution.py
@@ -166,15 +166,15 @@
     chunk = BLK // CHUNKS
     pieces = [pl.ds(n * chunk, chunk) for n in range(CHUNKS)]
     mine = [
-        remote(xw.at[2, rows], xw.at[1, rows], hs.at[n], hr.at[n], next1)
+        remote(xw.at[2, rows], xw.at[1, rows], hs.at[0], hr.at[n], next1)
         for n, rows in enumerate(pieces)
     ]
     onward = [
-        remote(xw.at[1, rows], xw.at[0, rows], hs.at[CHUNKS + n], hr.at[CHUNKS + n], next1)
+        remote(xw.at[1, rows], xw.at[0, rows], hs.at[1], hr.at[CHUNKS + n], next1)
         for n, rows in enumerate(pieces)
     ]
     times = [
-        remote(src, ts_near.at[n], hs.at[2 * CHUNKS + n], hr.at[2 * CHUNKS + n], next1)
+        remote(src, ts_near.at[n], hs.at[2 + n], hr.at[2 * CHUNKS + n], next1)
         for n, src in enumerate((stamps, ts_near.at[0]))
     ]
     weights = [
@@ -339,8 +339,8 @@
                     remote(
                         sources[stage].at[j, col, pl.ds(pl.multiple_of(there * piece, piece), piece)],
                         landing[stage].at[j, col, d - 1],
-                        rs_s.at[j, stage, col, d - 1],
-                        rs_r.at[j, stage, col, d - 1],
+                        rs_s.at[j, stage],
+                        rs_r.at[j, stage],
                         partner(axis, d),
                     )
                 )
@@ -370,13 +370,22 @@
                     remote(
                         red.at[col, j, here],
                         red.at[col, j, here],
-                        ag_s.at[j, stage, col, d - 1],
-                        ag_r.at[j, stage, col, d - 1],
+                        ag_s.at[j, stage],
+                        ag_r.at[j, stage],
                         partner(axis, d),
                     )
                 )
         return copies
 
+    def whole_scatter(j, stage):
+        ref = landing[stage].at[j]
+        return remote(ref, ref, rs_s.at[j, stage], rs_r.at[j, stage], sib)
+
+    def whole_spread(j, stage):
+        _, size, piece = place(stage, 0)
+        ref = red.at[:, j, pl.ds(0, (size - 1) * (piece // 8))]
+        return remote(ref, ref, ag_s.at[j, stage], ag_r.at[j, stage], sib)
+
     scatters = [[scatter(j, stage) for stage in range(3)] for j in range(2)]
     spreads = [[spread(j, stage) for stage in range(3)] for j in range(2)]
 
@@ -385,7 +394,7 @@
             copy.wait_recv()
 
     def next_scatter(j, stage):
-        arrived(scatters[j][stage])
+        whole_scatter(j, stage).wait_recv()
         for col in range(2):
             if stage < 2:
                 sources[stage + 1][j, col] = gathered(j, stage, col).astype(sources[stage + 1].dtype)
@@ -394,7 +403,7 @@
         begin(scatters[j][stage + 1] if stage < 2 else spreads[j][2])
 
     def next_spread(j, stage):
-        arrived(spreads[j][stage])
+        whole_spread(j, stage).wait_recv()
         begin(spreads[j][stage - 1])
 
     scale = 1.0 / math.sqrt(blocks * BLK)
@@ -457,12 +466,13 @@
     to_sib[1].start()
     next_spread(1, 1)
     arrived(to_sib)
-    arrived(spreads[0][0])
-    arrived(spreads[1][0])
-    sent = mine + onward + times + [decays] + weights + psends + terms[0] + terms[1] + to_sib
+    whole_spread(0, 0).wait_recv()
+    whole_spread(1, 0).wait_recv()
+    sent = [remote(xw.at[0], xw.at[0], hs.at[n], hr.at[n], next1) for n in range(2)]
+    sent += times + [decays] + weights + psends + terms[0] + terms[1] + to_sib
     for j in range(2):
         for stage in range(3):
-            sent += scatters[j][stage] + spreads[j][stage]
+            sent += [whole_scatter(j, stage), whole_spread(j, stage)]
     for copy in sent:
         copy.wait_send()
 
@@ -543,16 +553,16 @@
             V((2, D, BLK), BF16),
             V((2, D, BLK), F32),
             dma((9,)),
-            dma((2 * CHUNKS + 2,)),
+            dma((4,)),
             dma((2 * CHUNKS + 2,)),
             dma((5,)),
             dma((5,)),
             dma((2,)),
             dma((2,)),
-            dma((2, 3, 2, 7)),
-            dma((2, 3, 2, 7)),
-            dma((2, 3, 2, 7)),
-            dma((2, 3, 2, 7)),
+            dma((2, 3)),
+            dma((2, 3)),
+            dma((2, 3)),
+            dma((2, 3)),
             dma((2, 2)),
             dma((2, 2)),
             dma((2,)),

time: 60.1 us -> 57.1 us (0.950)
  Pallas kernels: 59 us -> 56 us
    pallas_call x1, Pallas kernels: 57.3 us -> 54.3 us  [shards(): pl.pallas_call(functools.partial(kernel, tm_size), out_shape=near, in_spe...]
where the time goes in v5:
time: 57.1 us; the launch traced here: 56.6 us
  Pallas kernels  56 us (98%)
  between operations  0.64 us (1%)
    pallas_call x1, Pallas kernels, shards(): pl.pallas_call(functools.partial(kernel, tm_size), out_shape=near, in_spe...  54.3 us
    pallas_call x1, Pallas kernels, shards(): pl.pallas_call(finish, out_shape=tuple((jax.ShapeDtypeStruct(shape, BF16...  1.71 us

profile of v5, /device:TPU:32, one launch (start us, length us, event | category | flops | bytes accessed | tf_op | source)
XLA Modules:
  0.0 56.6 jit_solution(3751598058338636759)
XLA Ops:
  0.6 54.3 %history_attention.1 = (bf16[2,256,512]{2,1,0:T(8,128)(2,1)S(1)}, bf16[2,256,512]{2,1,0:T(8,128)(2,1)S(1)}, bf16[2,2,128,8,128]{4,3,2,1,0:T(8,128)(2,1)S(1)}) custom-call(bf16[2,256,512]{2,1,0:T(8,128)(2,1)} %table.1, bf16[2,256,512]{2,1,0:T(8,128)(2,1)} %cot.1, s32[2,256]{1,0:T(2,128)} %stamps.1, s32[2,256]{1,0:T(2,128)} %starts.1, bf16[512,256]{1,0:T(8,128)(2,1)} %wq_in.1, ...), custom_call_target="tpu_custom_call" | custom-call | tf_op jit(solution)/shard_map/history_attention/pallas_call | solution.py:513
  54.9 1.7 %finish.1 = (bf16[2,256,512]{2,1,0:T(8,128)(2,1)}, bf16[2,256,512]{2,1,0:T(8,128)(2,1)}, f32[512,256]{1,0:T(8,128)}, f32[512,256]{1,0:T(8,128)}, f32[512,256]{1,0:T(8,128)}, /*index=5*/f32[256,512]{1,0:T(8,128)}) custom-call(bf16[2,256,512]{2,1,0:T(8,128)(2,1)S(1)} %get-tuple-element.9.mix, bf16[2,256,512]{2,1,0:T(8,128)(2,1)S(1)} %get-tuple-element.10.gtb, ...), custom_call_target="tpu_custom_call" | custom-call | tf_op jit(solution)/shard_map/finish/pallas_call | solution.py:578

commit v6 on v5

--- a/solution.py
+++ b/solution.py
@@ -60,6 +60,8 @@
     wo,
     mb,
     brow,
+    s_pre,
+    dp_pre,
     q_s,
     qT_s,
     k_s,
@@ -158,10 +160,10 @@
         axis, d, n = token
         pl.semaphore_signal(met.at[n], inc=1, device_id=partner(axis, d), device_id_type=MESH)
 
-    def hear(token):
-        pl.semaphore_wait(met.at[token[2]], 1)
-
-    tokens = ([("x", 1, 0), ("y", 1, 1), ("z", 1, 2), ("z", -1, 3)], [("z", 1, 4), ("z", -1, 5)], [("z", 1, 6)])
+    tokens = ([("x", 1, 0), ("y", 1, 0), ("z", 1, 0), ("z", -1, 0)], [("z", 1, 1), ("z", -1, 1)], [("z", 1, 2)])
+
+    def hear(n):
+        pl.semaphore_wait(met.at[n], len(tokens[n]))
 
     chunk = BLK // CHUNKS
     pieces = [pl.ds(n * chunk, chunk) for n in range(CHUNKS)]
@@ -178,10 +180,10 @@
         for n, src in enumerate((stamps, ts_near.at[0]))
     ]
     weights = [
-        remote(src.at[1], dst.at[0], ws.at[n], wr.at[n], sib)
+        remote(src.at[1], dst.at[0], ws.at[0], wr.at[0], sib)
         for n, (src, dst) in enumerate(((wq, wq), (wk, wk), (wv, wv), (wo, wo)))
     ]
-    decays = remote(dec_send, dec_recv, ws.at[4], wr.at[4], sib)
+    decays = remote(dec_send, dec_recv, ws.at[1], wr.at[1], sib)
     for copy in times[:1] + mine:
         copy.start()
     for token in tokens[0]:
@@ -231,59 +233,74 @@
     own_rows(1)
     keys_of(2, 1)
     xT[:, 2 * BLK :] = jnp.transpose(xw[2])
+
+    def side_row(ref, pos):
+        return jnp.where(pos // tm_size == 0, ref[0:1, :], ref[1:2, :])
+
+    own_times = side_row(ts_own, blk)
+    base = jnp.max(own_times, axis=1, keepdims=True)
+    inv_scale = 1.0 / math.sqrt(HD)
+
+    def columns(part):
+        return slice(part * BLK, (part + 1) * BLK)
+
+    def decay_terms(part, times_row):
+        rel = (times_row - base).astype(F32) * LOG2E
+        for h in range(4):
+            rate = (dec_recv, dec_send)[h // 2][h % 2 : h % 2 + 1, 0:1]
+            brow[h, :, columns(part)] = rel * rate
+
+    def scores(h, part):
+        raw = nt(q_s[h], k_s[h, columns(part), :]) * (inv_scale * LOG2E)
+        return raw + (mb[:, columns(part)] + brow[h, :, columns(part)])
+
+    def early(h, part):
+        s_pre[h, :, columns(part - 1)] = scores(h, part)
+        dp_pre[h, :, columns(part - 1)] = nt(do_s[h], v_s[h, columns(part), :])
+
+    all_weights = remote(psend, psend, ws.at[0], wr.at[0], sib)
+    all_weights.wait_recv()
+    decays.wait_recv()
+    own_rows(0)
+    keys_of(2, 0)
+    decay_terms(2, own_times)
     times[0].wait_recv()
     times[1].start()
-    for token in tokens[0]:
-        hear(token)
+    hear(0)
     for token in tokens[1]:
         tell(token)
     for n in range(CHUNKS):
         mine[n].wait_recv()
         onward[n].start()
-    for token in tokens[1]:
-        hear(token)
+        early(n, 2)
+    hear(1)
     for token in tokens[2]:
         tell(token)
     keys_of(1, 1)
+    keys_of(1, 0)
     xT[:, BLK : 2 * BLK] = jnp.transpose(xw[1])
-    for copy in weights:
-        copy.wait_recv()
-    own_rows(0)
-    keys_of(2, 0)
-    keys_of(1, 0)
-    for token in tokens[2]:
-        hear(token)
-    for copy in (times[1], decays):
-        copy.wait_recv()
+    decay_terms(1, side_row(ts_near.at[0], pos1))
+    for h in range(4):
+        early(h, 1)
+    hear(2)
+    times[1].wait_recv()
+    decay_terms(0, side_row(ts_near.at[1], pos2))
     for copy in onward:
         copy.wait_recv()
     keys_of(0, 0)
     keys_of(0, 1)
     xT[:, :BLK] = jnp.transpose(xw[0])
 
-    def side_row(ref, pos):
-        return jnp.where(pos // tm_size == 0, ref[0:1, :], ref[1:2, :])
-
-    own_times = side_row(ts_own, blk)
-    base = jnp.max(own_times, axis=1, keepdims=True)
-    rel = jnp.concatenate(
-        [side_row(ts_near.at[1], pos2), side_row(ts_near.at[0], pos1), own_times], axis=1
-    )
-    rel = (rel - base).astype(F32) * LOG2E
-    for j in range(2):
-        brow[j] = rel * dec_recv[j : j + 1, 0:1]
-        brow[2 + j] = rel * dec_send[j : j + 1, 0:1]
-
-    inv_scale = 1.0 / math.sqrt(HD)
     psends = [
-        remote(psend.at[j], precv.at[j], ps.at[j], pr.at[j], sib) for j in range(2)
+        remote(psend.at[j], precv.at[j], ps.at[0], pr.at[j], sib) for j in range(2)
     ]
 
     def products(t):
-        return nt(q_s[t], k_s[t]), nt(do_s[t], v_s[t])
+        return scores(t, 0), nt(do_s[t], v_s[t, :BLK, :])
 
     def softmax(t, s, dp):
-        s = s * (inv_scale * LOG2E) + (mb[...] + brow[t])
+        s = jnp.concatenate([s, s_pre[t]], axis=1)
+        dp = jnp.concatenate([dp, dp_pre[t]], axis=1)
         p = jnp.exp2(s - jnp.max(s, axis=-1, keepdims=True))
         p = p * (1.0 / jnp.sum(p, axis=-1, keepdims=True))
         delta = jnp.sum(p * dp, axis=-1, keepdims=True)
@@ -377,6 +394,26 @@
                 )
         return copies
 
+    def spread_last(j):
+        own, others = [], []
+        for col in range(2):
+            axis, size, _ = place(0, col)
+            second, count, piece = place(1, col)
+            base = coord[axis] * count
+            for e in range(count):
+                here = pl.ds((base + (coord[second] + e) % count) * (piece // 8), piece // 8)
+                for d in FARTHEST[size]:
+                    (others if e else own).append(
+                        remote(
+                            red.at[col, j, here],
+                            red.at[col, j, here],
+                            ag_s.at[j, 0],
+                            ag_r.at[j, 0],
+                            partner(axis, d),
+                        )
+                    )
+        return own, others
+
     def whole_scatter(j, stage):
         ref = landing[stage].at[j]
         return remote(ref, ref, rs_s.at[j, stage], rs_r.at[j, stage], sib)
@@ -387,7 +424,8 @@
         return remote(ref, ref, ag_s.at[j, stage], ag_r.at[j, stage], sib)
 
     scatters = [[scatter(j, stage) for stage in range(3)] for j in range(2)]
-    spreads = [[spread(j, stage) for stage in range(3)] for j in range(2)]
+    spreads = [[None, spread(j, 1), spread(j, 2)] for j in range(2)]
+    lasts = [spread_last(j) for j in range(2)]
 
     def arrived(copies):
         for copy in copies:
@@ -404,7 +442,9 @@
 
     def next_spread(j, stage):
         whole_spread(j, stage).wait_recv()
-        begin(spreads[j][stage - 1])
+        if stage == 2:
+            begin(spreads[j][1])
+        begin(lasts[j][2 - stage])
 
     scale = 1.0 / math.sqrt(blocks * BLK)
     turn = (0, 2, 1, 3)
@@ -423,7 +463,7 @@
 
     mix[c] = (nn(o_s[0], wo[0]) + nn(o_s[1], wo[1])).astype(BF16)
     to_sib = [
-        remote(ref.at[c], ref.at[c], ms.at[n], mr.at[n], sib) for n, ref in enumerate((mix, gtb))
+        remote(ref.at[c], ref.at[c], ms.at[0], mr.at[0], sib) for n, ref in enumerate((mix, gtb))
     ]
     to_sib[0].start()
     for part in range(3):
@@ -439,7 +479,7 @@
             ct_own[part - 1] = total
     terms = [
         [
-            remote(ct_send.at[n, rows], ct_recv.at[n, rows], cs.at[n, h], cr.at[n, h], prev1)
+            remote(ct_send.at[n, rows], ct_recv.at[n, rows], cs.at[0], cr.at[n, h], prev1)
             for h, rows in enumerate((every, pl.ds(BLK, BLK)))
         ]
         for n in range(2)
@@ -465,11 +505,14 @@
     gtb[c] = (gtq + jnp.transpose(ct_own[1] + ct_recv[1].astype(F32))).astype(BF16)
     to_sib[1].start()
     next_spread(1, 1)
-    arrived(to_sib)
+    both = remote(mix, mix, ms.at[0], mr.at[0], sib)
+    both.wait_recv()
     whole_spread(0, 0).wait_recv()
     whole_spread(1, 0).wait_recv()
     sent = [remote(xw.at[0], xw.at[0], hs.at[n], hr.at[n], next1) for n in range(2)]
-    sent += times + [decays] + weights + psends + terms[0] + terms[1] + to_sib
+    sent += times + [decays, all_weights, both]
+    sent += [remote(psend, psend, ps.at[0], pr.at[0], sib)]
+    sent += [remote(ct_send, ct_send, cs.at[0], cr.at[0, 0], prev1)]
     for j in range(2):
         for stage in range(3):
             sent += [whole_scatter(j, stage), whole_spread(j, stage)]
@@ -531,6 +574,8 @@
             V((2, BLK, D), BF16),
             V((BLK, WIN), F32),
             V((4, 1, WIN), F32),
+            V((4, BLK, 2 * BLK), F32),
+            V((4, BLK, 2 * BLK), F32),
             V((4, BLK, HD), BF16),
             V((4, HD, BLK), BF16),
             V((4, WIN, HD), BF16),
@@ -555,19 +600,19 @@
             dma((9,)),
             dma((4,)),
             dma((2 * CHUNKS + 2,)),
-            dma((5,)),
-            dma((5,)),
             dma((2,)),
+            dma((2,)),
+            dma((1,)),
             dma((2,)),
             dma((2, 3)),
             dma((2, 3)),
             dma((2, 3)),
             dma((2, 3)),
+            dma((1,)),
             dma((2, 2)),
-            dma((2, 2)),
-            dma((2,)),
-            dma((2,)),
-            pltpu.SemaphoreType.REGULAR((7,)),
+            dma((1,)),
+            dma((1,)),
+            pltpu.SemaphoreType.REGULAR((3,)),
         ],
         compiler_params=pltpu.CompilerParams(
             collective_id=0, has_side_effects=True, vmem_limit_bytes=58 * 1024 * 1024

time: 57.1 us -> 56.8 us (level)
  Pallas kernels: 56 us -> 55.2 us
    pallas_call x1, Pallas kernels: 54.3 us -> 53.5 us  [shards(): pl.pallas_call(functools.partial(kernel, tm_size), out_shape=near, in_spe...]
where the time goes in v6:
time: 56.8 us; the launch traced here: 55.9 us
  Pallas kernels  55.2 us (97%)
  between operations  0.64 us (1%)
    pallas_call x1, Pallas kernels, shards(): pl.pallas_call(functools.partial(kernel, tm_size), out_shape=near, in_spe...  53.5 us
    pallas_call x1, Pallas kernels, shards(): pl.pallas_call(finish, out_shape=tuple((jax.ShapeDtypeStruct(shape, BF16...  1.71 us

profile of v6, /device:TPU:32, one launch (start us, length us, event | category | flops | bytes accessed | tf_op | source)
XLA Modules:
  0.0 55.9 jit_solution(5301110555675734979)
XLA Ops:
  0.6 53.5 %history_attention.1 = (bf16[2,256,512]{2,1,0:T(8,128)(2,1)S(1)}, bf16[2,256,512]{2,1,0:T(8,128)(2,1)S(1)}, bf16[2,2,128,8,128]{4,3,2,1,0:T(8,128)(2,1)S(1)}) custom-call(bf16[2,256,512]{2,1,0:T(8,128)(2,1)} %table.1, bf16[2,256,512]{2,1,0:T(8,128)(2,1)} %cot.1, s32[2,256]{1,0:T(2,128)} %stamps.1, s32[2,256]{1,0:T(2,128)} %starts.1, bf16[512,256]{1,0:T(8,128)(2,1)} %wq_in.1, ...), custom_call_target="tpu_custom_call" | custom-call | tf_op jit(solution)/shard_map/history_attention/pallas_call | solution.py:556
  54.2 1.7 %finish.1 = (bf16[2,256,512]{2,1,0:T(8,128)(2,1)}, bf16[2,256,512]{2,1,0:T(8,128)(2,1)}, f32[512,256]{1,0:T(8,128)}, f32[512,256]{1,0:T(8,128)}, f32[512,256]{1,0:T(8,128)}, /*index=5*/f32[256,512]{1,0:T(8,128)}) custom-call(bf16[2,256,512]{2,1,0:T(8,128)(2,1)S(1)} %get-tuple-element.9.mix, bf16[2,256,512]{2,1,0:T(8,128)(2,1)S(1)} %get-tuple-element.10.gtb, ...), custom_call_target="tpu_custom_call" | custom-call | tf_op jit(solution)/shard_map/finish/pallas_call | solution.py:623

commit v7 on v6

--- a/solution.py
+++ b/solution.py
@@ -77,6 +77,8 @@
     b0,
     b1,
     b2,
+    b1_exact,
+    b2_exact,
     rc0,
     rc1,
     rc2,
@@ -340,6 +342,7 @@
 
     sources = (b0, b1, b2)
     landing = (rc0, rc1, rc2)
+    exact = (b1_exact, b2_exact)
     rows_at = (2 * D, D // 2, D // 8)
 
     def place(stage, col):
@@ -352,9 +355,10 @@
             axis, size, piece = place(stage, col)
             for d in FARTHEST[size]:
                 there = (coord[axis] + d) % size
+                rows = there if stage == 2 else pl.ds(pl.multiple_of(there * piece, piece), piece)
                 copies.append(
                     remote(
-                        sources[stage].at[j, col, pl.ds(pl.multiple_of(there * piece, piece), piece)],
+                        sources[stage].at[j, col, rows],
                         landing[stage].at[j, col, d - 1],
                         rs_s.at[j, stage],
                         rs_r.at[j, stage],
@@ -365,7 +369,11 @@
 
     def gathered(j, stage, col):
         axis, size, piece = place(stage, col)
-        total = sources[stage][j, col, pl.ds(pl.multiple_of(coord[axis] * piece, piece), piece), :].astype(F32)
+        if stage == 0:
+            here = (2 * col + coord[axis] // 2, pl.ds(pl.multiple_of(coord[axis] % 2 * piece, piece), piece))
+            total = pown[j, here[0], here[1], :] + precv[j, here[0], here[1], :].astype(F32)
+        else:
+            total = exact[stage - 1][j, col, pl.ds(pl.multiple_of(coord[axis] * piece, piece), piece), :]
         for d in range(1, size):
             total = total + landing[stage][j, col, d - 1].astype(F32)
         return total
@@ -435,7 +443,11 @@
         whole_scatter(j, stage).wait_recv()
         for col in range(2):
             if stage < 2:
-                sources[stage + 1][j, col] = gathered(j, stage, col).astype(sources[stage + 1].dtype)
+                total = gathered(j, stage, col)
+                exact[stage][j, col] = total
+                if stage == 1:
+                    total = total.reshape(NZ, 8, 128)
+                sources[stage + 1][j, col] = total.astype(BF16)
             else:
                 red[col, j, first_owner(2, col)] = (gathered(j, 2, col) * scale).astype(BF16)
         begin(scatters[j][stage + 1] if stage < 2 else spreads[j][2])
@@ -590,10 +602,12 @@
             V((2, 4, D, 128), F32),
             V((2, 2, 2 * D, 128), BF16),
             V((2, 2, D // 2, 128), BF16),
+            V((2, 2, NZ, 8, 128), BF16),
+            V((2, 2, D // 2, 128), F32),
             V((2, 2, D // 8, 128), F32),
             V((2, 2, 3, D // 2, 128), BF16),
             V((2, 2, 3, D // 8, 128), BF16),
-            V((2, 2, 7, 8, 128), F32),
+            V((2, 2, 7, 8, 128), BF16),
             V((2, D, BLK), BF16),
             V((2, D, BLK), BF16),
             V((2, D, BLK), F32),

time: 56.8 us -> 55.8 us (0.982); the launches traced: 55.9 us -> 55.7 us
  no operation moved by 1% of the time
where the time goes in v7:
time: 55.8 us; the launch traced here: 55.7 us
  Pallas kernels  55.1 us (99%)
  between operations  0.64 us (1%)
    pallas_call x1, Pallas kernels, shards(): pl.pallas_call(functools.partial(kernel, tm_size), out_shape=near, in_spe...  53.4 us
    pallas_call x1, Pallas kernels, shards(): pl.pallas_call(finish, out_shape=tuple((jax.ShapeDtypeStruct(shape, BF16...  1.71 us

profile of v7, /device:TPU:32, one launch (start us, length us, event | category | flops | bytes accessed | tf_op | source)
XLA Modules:
  0.0 55.7 jit_solution(13757410506777044867)
XLA Ops:
  0.6 53.4 %history_attention.1 = (bf16[2,256,512]{2,1,0:T(8,128)(2,1)S(1)}, bf16[2,256,512]{2,1,0:T(8,128)(2,1)S(1)}, bf16[2,2,128,8,128]{4,3,2,1,0:T(8,128)(2,1)S(1)}) custom-call(bf16[2,256,512]{2,1,0:T(8,128)(2,1)} %table.1, bf16[2,256,512]{2,1,0:T(8,128)(2,1)} %cot.1, s32[2,256]{1,0:T(2,128)} %stamps.1, s32[2,256]{1,0:T(2,128)} %starts.1, bf16[512,256]{1,0:T(8,128)(2,1)} %wq_in.1, ...), custom_call_target="tpu_custom_call" | custom-call | tf_op jit(solution)/shard_map/history_attention/pallas_call | solution.py:568
  54.0 1.7 %finish.1 = (bf16[2,256,512]{2,1,0:T(8,128)(2,1)}, bf16[2,256,512]{2,1,0:T(8,128)(2,1)}, f32[512,256]{1,0:T(8,128)}, f32[512,256]{1,0:T(8,128)}, f32[512,256]{1,0:T(8,128)}, /*index=5*/f32[256,512]{1,0:T(8,128)}) custom-call(bf16[2,256,512]{2,1,0:T(8,128)(2,1)S(1)} %get-tuple-element.9.mix, bf16[2,256,512]{2,1,0:T(8,128)(2,1)S(1)} %get-tuple-element.10.gtb, ...), custom_call_target="tpu_custom_call" | custom-call | tf_op jit(solution)/shard_map/finish/pallas_call | solution.py:637

commit v8 on v7

--- a/solution.py
+++ b/solution.py
@@ -13,7 +13,7 @@
 WIN = 3 * BLK
 D = 512
 NX, NY, NZ = 4, 4, 8
-CHUNKS = 4
+CHUNKS = 8
 LOG2E = 1.4426950408889634
 MESH = pl.DeviceIdType.MESH
 F32 = jnp.float32
@@ -274,7 +274,8 @@
     for n in range(CHUNKS):
         mine[n].wait_recv()
         onward[n].start()
-        early(n, 2)
+        if n % 2:
+            early(n // 2, 2)
     hear(1)
     for token in tokens[2]:
         tell(token)
@@ -504,12 +505,18 @@
     begin(terms[0])
     next_scatter(1, 1)
     next_scatter(0, 2)
-    for h in range(2):
-        terms[0][h].wait_recv()
-        rows = slice(h * BLK, (h + 1) * BLK)
-        ct_send[1, rows, :] = (ct_own[0, rows, :] + ct_recv[0, rows, :].astype(F32)).astype(BF16)
-        terms[1][h].start()
+    late = coord["y"] == (1 - c) * (NY - 1)
+
+    def relay_terms():
+        for h in range(2):
+            terms[0][h].wait_recv()
+            rows = slice(h * BLK, (h + 1) * BLK)
+            ct_send[1, rows, :] = (ct_own[0, rows, :] + ct_recv[0, rows, :].astype(F32)).astype(BF16)
+            terms[1][h].start()
+
+    pl.when(jnp.logical_not(late))(relay_terms)
     next_scatter(1, 2)
+    pl.when(late)(relay_terms)
     next_spread(0, 2)
     next_spread(1, 2)
     next_spread(0, 1)

time: 55.8 us -> 55.6 us (level)
  no operation moved by 1% of the time
where the time goes in v8:
time: 55.6 us; the launch traced here: 55.5 us
  Pallas kernels  54.9 us (99%)
  between operations  0.64 us (1%)
    pallas_call x1, Pallas kernels, shards(): pl.pallas_call(functools.partial(kernel, tm_size), out_shape=near, in_spe...  53.2 us
    pallas_call x1, Pallas kernels, shards(): pl.pallas_call(finish, out_shape=tuple((jax.ShapeDtypeStruct(shape, BF16...  1.71 us

profile of v8, /device:TPU:32, one launch (start us, length us, event | category | flops | bytes accessed | tf_op | source)
XLA Modules:
  0.0 55.5 jit_solution(17997699810414971077)
XLA Ops:
  0.6 53.2 %history_attention.1 = (bf16[2,256,512]{2,1,0:T(8,128)(2,1)S(1)}, bf16[2,256,512]{2,1,0:T(8,128)(2,1)S(1)}, bf16[2,2,128,8,128]{4,3,2,1,0:T(8,128)(2,1)S(1)}) custom-call(bf16[2,256,512]{2,1,0:T(8,128)(2,1)} %table.1, bf16[2,256,512]{2,1,0:T(8,128)(2,1)} %cot.1, s32[2,256]{1,0:T(2,128)} %stamps.1, s32[2,256]{1,0:T(2,128)} %starts.1, bf16[512,256]{1,0:T(8,128)(2,1)} %wq_in.1, ...), custom_call_target="tpu_custom_call" | custom-call | tf_op jit(solution)/shard_map/history_attention/pallas_call | solution.py:575
  53.8 1.7 %finish.1 = (bf16[2,256,512]{2,1,0:T(8,128)(2,1)}, bf16[2,256,512]{2,1,0:T(8,128)(2,1)}, f32[512,256]{1,0:T(8,128)}, f32[512,256]{1,0:T(8,128)}, f32[512,256]{1,0:T(8,128)}, /*index=5*/f32[256,512]{1,0:T(8,128)}) custom-call(bf16[2,256,512]{2,1,0:T(8,128)(2,1)S(1)} %get-tuple-element.9.mix, bf16[2,256,512]{2,1,0:T(8,128)(2,1)S(1)} %get-tuple-element.10.gtb, ...), custom_call_target="tpu_custom_call" | custom-call | tf_op jit(solution)/shard_map/finish/pallas_call | solution.py:644

commit v9 on v8

--- a/solution.py
+++ b/solution.py
@@ -466,9 +466,9 @@
         later = products(turn[step + 1]) if step < 3 else None
         if step > 0:
             weight_grads(turn[step - 1])
-        pb, ds = softmax(turn[step], *now)
         if step > 0:
             pass_on(step - 1)
+        pb, ds = softmax(turn[step], *now)
         attention(turn[step], pb, ds)
         now = later
     weight_grads(turn[3])

time: 55.6 us -> 55.7 us (level)
  no operation moved by 1% of the time
where the time goes in v9:
time: 55.7 us; the launch traced here: 55.6 us
  Pallas kernels  54.9 us (99%)
  between operations  0.64 us (1%)
    pallas_call x1, Pallas kernels, shards(): pl.pallas_call(functools.partial(kernel, tm_size), out_shape=near, in_spe...  53.2 us
    pallas_call x1, Pallas kernels, shards(): pl.pallas_call(finish, out_shape=tuple((jax.ShapeDtypeStruct(shape, BF16...  1.71 us

profile of v9, /device:TPU:32, one launch (start us, length us, event | category | flops | bytes accessed | tf_op | source)
XLA Modules:
  0.0 55.6 jit_solution(14315770963767726130)
XLA Ops:
  0.6 53.2 %history_attention.1 = (bf16[2,256,512]{2,1,0:T(8,128)(2,1)S(1)}, bf16[2,256,512]{2,1,0:T(8,128)(2,1)S(1)}, bf16[2,2,128,8,128]{4,3,2,1,0:T(8,128)(2,1)S(1)}) custom-call(bf16[2,256,512]{2,1,0:T(8,128)(2,1)} %table.1, bf16[2,256,512]{2,1,0:T(8,128)(2,1)} %cot.1, s32[2,256]{1,0:T(2,128)} %stamps.1, s32[2,256]{1,0:T(2,128)} %starts.1, bf16[512,256]{1,0:T(8,128)(2,1)} %wq_in.1, ...), custom_call_target="tpu_custom_call" | custom-call | tf_op jit(solution)/shard_map/history_attention/pallas_call | solution.py:575
  53.9 1.7 %finish.1 = (bf16[2,256,512]{2,1,0:T(8,128)(2,1)}, bf16[2,256,512]{2,1,0:T(8,128)(2,1)}, f32[512,256]{1,0:T(8,128)}, f32[512,256]{1,0:T(8,128)}, f32[512,256]{1,0:T(8,128)}, /*index=5*/f32[256,512]{1,0:T(8,128)}) custom-call(bf16[2,256,512]{2,1,0:T(8,128)(2,1)S(1)} %get-tuple-element.9.mix, bf16[2,256,512]{2,1,0:T(8,128)(2,1)S(1)} %get-tuple-element.10.gtb, ...), custom_call_target="tpu_custom_call" | custom-call | tf_op jit(solution)/shard_map/finish/pallas_call | solution.py:644
